TPU v7x, 256 devices: a whole 4x4x8 slice. The times are simulated.
256 devices in a mesh: gx: 16 (over z, x_hi), gy: 16 (over x_lo, y, core).
Axes of the slice: x: 4 (x_hi: 2, x_lo: 2; x = x_hi * 2 + x_lo), y: 4, z: 8, core: 2. Of those that a mesh axis runs over, the one named last changes fastest.
Arguments:
- density: float32 [64, 256, 128], P('gx', 'gy'), may hold values from 0.05 to 1
- passive: int32 [64, 256, 128], P('gx', 'gy'), may hold values 0 or 1
- element_load: float32 [24, 16, 64, 32], P(None, 'gx', 'gy'), may hold values from -5 to 5
Outputs:
- physical: float32 [64, 256, 128], P('gx', 'gy')
- coarse_solution: float32 [3, 16, 65, 33], P(None, 'gx')
All inputs are finite; a program needn't handle non-finite values. No bound on the sum of `passive` on one device may be relied on, other than what follows from the above.
Results may differ from a plain program's by a relative error of at most 0.0001.
Values sent between devices are 32-bit elements; how exact they have to be, the bound alone decides.
A program may use at most 128 MiB of HBM per device.

v0:
```python
import math

import jax
import jax.numpy as jnp
import numpy as np
from jax import lax
from jax.sharding import PartitionSpec as P

SWEEPS = 6


RELAX = 0.6
YOUNG_MIN = 0.001
HIGHEST = lax.Precision.HIGHEST


def padded_2(cells, sides, width):
    for axis, dim in sides:
        count = lax.axis_size(axis)
        ends = count - 1
        head = lax.slice_in_dim(cells, 0, width, axis=dim)
        tail = lax.slice_in_dim(cells, cells.shape[dim] - width, cells.shape[dim], axis=dim)
        cells = jnp.concatenate(
            [
                lax.ppermute(tail, axis, [(i, (i + 1) % count) for i in range(ends)]),
                cells,
                lax.ppermute(head, axis, [((i + 1) % count, i) for i in range(ends)]),
            ],
            axis=dim,
        )
    return cells


def from_behind(value, axis, by):
    length = lax.axis_size(axis)
    pairs = [(i, i + by) for i in range(length) if 0 <= i + by < length]
    return lax.ppermute(value, axis, pairs)


def corner_bits(corner_id):
    return [corner_id >> 2 & 1, corner_id >> 1 & 1, corner_id & 1]


def stiffness_table():
    poisson = 0.3
    lame_first = poisson / ((1.0 + poisson) * (1.0 - 2.0 * poisson))
    lame_shear = 1.0 / (2.0 * (1.0 + poisson))
    elastic = np.zeros((6, 6))
    elastic[:3, :3] = lame_first
    for dim_index in range(3):
        elastic[dim_index, dim_index] += 2.0 * lame_shear
        elastic[3 + dim_index, 3 + dim_index] = lame_shear
    corners = np.array([corner_bits(corner_id) for corner_id in range(8)])
    gauss_points = [0.5 - 0.5 / math.sqrt(3.0), 0.5 + 0.5 / math.sqrt(3.0)]
    matrix_sum = np.zeros((24, 24))
    for gauss_x in gauss_points:
        for gauss_y in gauss_points:
            for gauss_z in gauss_points:
                location = np.array([gauss_x, gauss_y, gauss_z])
                shape_values = np.where(corners == 1, location, 1.0 - location)
                gradients = np.zeros((8, 3))
                for dim_index in range(3):
                    slope_sign = np.where(corners[:, dim_index] == 1, 1.0, -1.0)
                    others = (
                        shape_values[:, (dim_index + 1) % 3] * shape_values[:, (dim_index + 2) % 3]
                    )
                    gradients[:, dim_index] = slope_sign * others
                strain = np.zeros((6, 24))
                for dim_index in range(3):
                    strain[dim_index, 8 * dim_index : 8 * dim_index + 8] = gradients[:, dim_index]
                for shear_index, (dim_p, dim_q) in enumerate([(0, 1), (1, 2), (0, 2)]):
                    strain[3 + shear_index, 8 * dim_p : 8 * dim_p + 8] = gradients[:, dim_q]
                    strain[3 + shear_index, 8 * dim_q : 8 * dim_q + 8] = gradients[:, dim_p]
                matrix_sum = matrix_sum + 0.125 * strain.T @ elastic @ strain
    return matrix_sum


def prolong_table():
    matrix_set = np.zeros((8, 24, 24))
    for child_id in range(8):
        child_bits = corner_bits(child_id)
        for fine_node in range(8):
            fine_bits = corner_bits(fine_node)
            for coarse_node in range(8):
                coarse_bits = corner_bits(coarse_node)
                factor = 1.0
                for dim_index in range(3):
                    position = (child_bits[dim_index] + fine_bits[dim_index]) / 2.0
                    factor = factor * (position if coarse_bits[dim_index] == 1 else 1.0 - position)
                for component in range(3):
                    matrix_set[child_id, 8 * component + fine_node, 8 * component + coarse_node] = (
                        factor
                    )
    return matrix_set


def second_table():
    prolong = prolong_table()
    stiffness = stiffness_table()
    tables = []
    for outer_id in range(8):
        for inner_id in range(8):
            inner = prolong[inner_id].T @ stiffness @ prolong[inner_id]
            tables.append(prolong[outer_id].T @ inner @ prolong[outer_id])
    return np.stack(tables, axis=-1).reshape(576, 64)


def smooth(padded):
    size_x = padded.shape[0] - 2
    size_y = padded.shape[1] - 2
    size_z = padded.shape[2] - 2
    summed = jnp.zeros((size_x, size_y, size_z), padded.dtype)
    for off_x in range(3):
        for off_y in range(3):
            for off_z in range(3):
                steps_sq = (off_x - 1) ** 2 + (off_y - 1) ** 2 + (off_z - 1) ** 2
                if steps_sq == 3:
                    continue
                weight = 1.5 - math.sqrt(steps_sq)
                summed = (
                    summed
                    + weight
                    * padded[off_x : off_x + size_x, off_y : off_y + size_y, off_z : off_z + size_z]
                )
    return summed


def element_dofs(node_values):
    size_x = node_values.shape[1] - 1
    size_y = node_values.shape[2] - 1
    size_z = node_values.shape[3] - 1
    pieces = []
    for corner_id in range(8):
        offsets = corner_bits(corner_id)
        pieces.append(
            node_values[
                :,
                offsets[0] : offsets[0] + size_x,
                offsets[1] : offsets[1] + size_y,
                offsets[2] : offsets[2] + size_z,
            ]
        )
    return jnp.stack(pieces, axis=1).reshape(24, size_x, size_y, size_z)


def scatter_nodes(element_values):
    size_x, size_y, size_z = element_values.shape[1:]
    pieces = element_values.reshape(3, 8, size_x, size_y, size_z)
    summed = None
    for corner_id in range(8):
        offsets = corner_bits(corner_id)
        placed = jnp.pad(
            pieces[:, corner_id],
            (
                (0, 0),
                (offsets[0], 1 - offsets[0]),
                (offsets[1], 1 - offsets[1]),
                (offsets[2], 1 - offsets[2]),
            ),
        )
        summed = placed if summed is None else summed + placed
    return summed


def apply_blocks(blocks, node_values):
    local = jnp.einsum("abxyz,bxyz->axyz", blocks, element_dofs(node_values), precision=HIGHEST)
    return scatter_nodes(local)


def body(density, passive, element_load):
    size_x, size_y, size_z = density.shape
    padded = padded_2(density, (("gx", 0), ("gy", 1)), 1)
    padded = jnp.pad(padded, ((0, 0), (0, 0), (1, 1)))
    grid_shape = (size_x + 2, size_y + 2, size_z + 2)
    index_x = lax.broadcasted_iota(jnp.int32, grid_shape, 0)
    index_y = lax.broadcasted_iota(jnp.int32, grid_shape, 1)
    index_z = lax.broadcasted_iota(jnp.int32, grid_shape, 2)
    place_x = lax.axis_index("gx")
    place_y = lax.axis_index("gy")
    inside = ((index_x > 0) | (place_x > 0)) & (
        (index_x < size_x + 1) | (place_x < lax.axis_size("gx") - 1)
    )
    inside = (
        inside
        & ((index_y > 0) | (place_y > 0))
        & ((index_y < size_y + 1) | (place_y < lax.axis_size("gy") - 1))
    )
    inside = inside & (index_z > 0) & (index_z < size_z + 1)
    filtered = smooth(padded) / smooth(inside.astype(jnp.float32))
    physical = jnp.where(passive == 1, jnp.ones_like(filtered), filtered)
    modulus = YOUNG_MIN + (1.0 - YOUNG_MIN) * physical**3
    table = jnp.asarray(second_table(), jnp.float32)
    quarter_x, quarter_y, quarter_z = (size_x // 4, size_y // 4, size_z // 4)
    grouped = (
        modulus.reshape(quarter_x, 2, 2, quarter_y, 2, 2, quarter_z, 2, 2)
        .transpose(1, 4, 7, 2, 5, 8, 0, 3, 6)
        .reshape(64, quarter_x, quarter_y, quarter_z)
    )
    level_two = jnp.dot(table, grouped.reshape(64, -1), precision=HIGHEST)
    outgoing = level_two.reshape(576, quarter_x, quarter_y, quarter_z)
    stored, load_blocks = (
        lax.all_gather(outgoing, "gy", axis=2, tiled=True),
        lax.all_gather(element_load, "gy", axis=2, tiled=True),
    )
    layers, column_y, column_z = stored.shape[1:]
    blocks = stored.reshape(24, 24, layers, column_y, column_z)
    diagonal_part = scatter_nodes(stored[::25])
    right_part = scatter_nodes(load_blocks)
    incoming_right, incoming_diagonal = from_behind(
        (right_part[:, -1:], diagonal_part[:, -1:]), "gx", 1
    )
    right_side = jnp.concatenate([right_part[:, :1] + incoming_right, right_part[:, 1:-1]], axis=1)
    diagonal = jnp.concatenate(
        [diagonal_part[:, :1] + incoming_diagonal, diagonal_part[:, 1:-1]], axis=1
    )
    solution = RELAX * right_side / diagonal
    for turn_index in range(SWEEPS - 1):
        beyond = from_behind(solution, "gx", -1)
        summed_terms = apply_blocks(blocks, jnp.concatenate([solution, beyond], axis=1))
        arriving = from_behind(summed_terms[:, -1:], "gx", 1)
        product = jnp.concatenate([summed_terms[:, :1] + arriving, summed_terms[:, 1:-1]], axis=1)
        solution = solution + RELAX * (right_side - product) / diagonal
    return (physical, solution)


def solution(mesh):
    return jax.shard_map(
        body,
        mesh=mesh,
        in_specs=(P("gx", "gy", None), P("gx", "gy", None), P(None, "gx", "gy", None)),
        out_specs=(P("gx", "gy", None), P(None, "gx", None, None)),
        check_vma=False,
    )
```

profile of v0, /device:TPU:102, one launch (start us, length us, event | category | flops | bytes accessed | tf_op | source)
XLA Modules:
  0.0 238.5 jit_solution(2698838539151475136)
XLA Ops:
  7.9 5.9 %collective-permute-start = (f32[1,16,128]{2,1,0:T(8,128)S(1)}, f32[1,16,128]{2,1,0:T(8,128)S(1)}, u32[]{:S(2)}, u32[]{:S(2)}) collective-permute-start(f32[1,16,128]{2,1,0:T(8,128)S(1)} %get-tuple-element.72), channel_id=1, source_target_pairs={{0,16},{16,32},{32,48},{48,64},{64,80},{80,96},{96,112},{112,128},... | collective-permute-start | bytes 24584 | tf_op jit(solution)/shard_map/ppermute | solution.py:25
  13.8 1.9 collective-permute-start.1
  16.6 6.4 %collective-permute-done.1 = f32[1,16,128]{2,1,0:T(8,128)S(1)} collective-permute-done((f32[1,16,128]{2,1,0:T(8,128)S(1)}, f32[1,16,128]{2,1,0:T(8,128)S(1)}, u32[]{:S(2)}, u32[]{:S(2)}) %collective-permute-start.1) | collective-permute-done | bytes 8224 | tf_op jit(solution)/shard_map/ppermute | solution.py:27
  23.0 2.3 collective-permute-start.3
  25.3 2.0 collective-permute-start.2
  27.4 4.9 %collective-permute-done.2 = f32[6,1,128]{2,1,0:T(1,128)S(1)} collective-permute-done((f32[6,1,128]{2,1,0:T(1,128)S(1)}, f32[6,1,128]{2,1,0:T(1,128)S(1)}, u32[]{:S(2)}, u32[]{:S(2)}) %collective-permute-start.2) | collective-permute-done | bytes 3104 | tf_op jit(solution)/shard_map/ppermute | solution.py:25
  34.1 3.2 %reshape.75 = f32[1,2,2,4,2,2,32,2,2]{8,7,6,5,4,3,2,1,0:T(2,128)S(1)} reshape(f32[4,16,128]{2,1,0:T(8,128)S(1)} %get-tuple-element.11) | data formatting | bytes 65536 | tf_op jit(solution)/shard_map/reshape | solution.py:195
  38.7 2.2 fusion.74
  41.7 20.6 %all_gather.6 = f32[24,1,64,32]{3,0,1,2:T(8,128)S(1)} all-gather(f32[24,1,4,32]{3,0,1,2:T(8,128)S(1)} %copy.179), channel_id=1, replica_groups=mesh['gx'=16,'gy'=16] {'gy'}, dimensions={2}, use_global_device_ids=true | all-gather | bytes 208896 | tf_op jit(solution)/shard_map/all_gather | solution.py:203
  62.7 3.3 %collective-permute-start.4 = (f32[3,1,65,33]{2,3,0,1:T(8,128)S(1)}, f32[3,1,65,33]{2,3,0,1:T(8,128)S(1)}, u32[]{:S(2)}, u32[]{:S(2)}) collective-permute-start(f32[3,1,65,33]{2,3,0,1:T(8,128)S(1)} %slice.677), channel_id=1, source_target_pairs={{0,16},{16,32},{32,48},{48,64},{64,80},{80,96},{96,112},{112,128},... | collective-permute-start | bytes 77228 | tf_op jit(solution)/shard_map/ppermute | solution.py:37
  66.0 15.2 %all-gather.2.cloned.1.call-done = f32[576,1,64,32]{0,3,1,2:T(8,128)} async-done(((f32[576,1,4,32]{0,3,1,2:T(8,128)}), f32[576,1,64,32]{0,3,1,2:T(8,128)}) %all-gather.2.cloned.1.call-update) | async-done | bytes 4718608 | tf_op jit(solution)/shard_map/all_gather | solution.py:202
  81.2 33.1 %slice.528 = f32[24,1,64,32]{0,3,1,2:T(8,128)S(1)} slice(f32[576,1,64,32]{0,3,1,2:T(8,128)} %all-gather.2.cloned.1.call-done), slice={[0:576:25], [0:1:1], [0:64:1], [0:32:1]} | slice | bytes 393216 | tf_op jit(solution)/shard_map/slice | solution.py:207
  115.2 5.0 %collective-permute-start.5 = (f32[3,1,65,33]{2,3,0,1:T(8,128)S(1)}, f32[3,1,65,33]{2,3,0,1:T(8,128)S(1)}, u32[]{:S(2)}, u32[]{:S(2)}) collective-permute-start(f32[3,1,65,33]{2,3,0,1:T(8,128)S(1)} %slice.687), channel_id=1, source_target_pairs={{0,16},{16,32},{32,48},{48,64},{64,80},{80,96},{96,112},{112,128},... | collective-permute-start | bytes 77228 | tf_op jit(solution)/shard_map/ppermute | solution.py:37
  120.2 10.8 %copy.278 = f32[576,1,64,32]{2,3,0,1:T(8,128)} copy(f32[576,1,64,32]{0,3,1,2:T(8,128)} %all-gather.2.cloned.1.call-done) | data formatting | bytes 9437184
  131.0 2.8 %collective-permute-start.6 = (f32[3,1,65,33]{2,3,0,1:T(8,128)S(1)}, f32[3,1,65,33]{2,3,0,1:T(8,128)S(1)}, u32[]{:S(2)}, u32[]{:S(2)}) collective-permute-start(f32[3,1,65,33]{2,3,0,1:T(8,128)S(1)} %get-tuple-element.8), channel_id=1, source_target_pairs={{16,0},{32,16},{48,32},{64,48},{80,64},{96,80},{112,96},{128,112},... | collective-permute-start | bytes 77228 | tf_op jit(solution)/shard_map/ppermute | solution.py:37
  134.0 7.1 %collective-permute-done.6 = f32[3,1,65,33]{2,3,0,1:T(8,128)S(1)} collective-permute-done((f32[3,1,65,33]{2,3,0,1:T(8,128)S(1)}, f32[3,1,65,33]{2,3,0,1:T(8,128)S(1)}, u32[]{:S(2)}, u32[]{:S(2)}) %collective-permute-start.6) | collective-permute-done | bytes 25772 | tf_op jit(solution)/shard_map/ppermute | solution.py:37
  141.2 5.0 %multiply_reduce_fusion.4 = f32[64,32,24]{0,1,2:T(8,128)S(1)} fusion(f32[64,32,24,24]{0,1,2,3:T(8,128)} %bitcast.448, f32[64,32,24]{0,1,2:T(8,128)S(1)} %bitcast.460), kind=kLoop, calls=%fused_computation.4 | loop fusion | flops 2310144 | bytes 5111808 | tf_op jit(solution)/shard_map/abxyz,bxyz->axyz/dot_general | solution.py:166
  146.4 2.1 collective-permute-start.7
  148.5 5.5 %collective-permute-done.7 = f32[3,1,65,33]{2,3,0,1:T(8,128)S(1)} collective-permute-done((f32[3,1,65,33]{2,3,0,1:T(8,128)S(1)}, f32[3,1,65,33]{2,3,0,1:T(8,128)S(1)}, u32[]{:S(2)}, u32[]{:S(2)}) %collective-permute-start.7) | collective-permute-done | bytes 25772 | tf_op jit(solution)/shard_map/ppermute | solution.py:37
  154.1 1.9 collective-permute-start.8
  156.2 7.6 %collective-permute-done.8 = f32[3,1,65,33]{2,3,0,1:T(8,128)S(1)} collective-permute-done((f32[3,1,65,33]{2,3,0,1:T(8,128)S(1)}, f32[3,1,65,33]{2,3,0,1:T(8,128)S(1)}, u32[]{:S(2)}, u32[]{:S(2)}) %collective-permute-start.8) | collective-permute-done | bytes 25772 | tf_op jit(solution)/shard_map/ppermute | solution.py:37
  165.5 2.1 collective-permute-start.9
  167.6 5.5 %collective-permute-done.9 = f32[3,1,65,33]{2,3,0,1:T(8,128)S(1)} collective-permute-done((f32[3,1,65,33]{2,3,0,1:T(8,128)S(1)}, f32[3,1,65,33]{2,3,0,1:T(8,128)S(1)}, u32[]{:S(2)}, u32[]{:S(2)}) %collective-permute-start.9) | collective-permute-done | bytes 25772 | tf_op jit(solution)/shard_map/ppermute | solution.py:37
  175.2 7.6 %collective-permute-done.10 = f32[3,1,65,33]{2,3,0,1:T(8,128)S(1)} collective-permute-done((f32[3,1,65,33]{2,3,0,1:T(8,128)S(1)}, f32[3,1,65,33]{2,3,0,1:T(8,128)S(1)}, u32[]{:S(2)}, u32[]{:S(2)}) %collective-permute-start.10) | collective-permute-done | bytes 25772 | tf_op jit(solution)/shard_map/ppermute | solution.py:37
  184.5 2.1 collective-permute-start.11
  186.6 5.5 %collective-permute-done.11 = f32[3,1,65,33]{2,3,0,1:T(8,128)S(1)} collective-permute-done((f32[3,1,65,33]{2,3,0,1:T(8,128)S(1)}, f32[3,1,65,33]{2,3,0,1:T(8,128)S(1)}, u32[]{:S(2)}, u32[]{:S(2)}) %collective-permute-start.11) | collective-permute-done | bytes 25772 | tf_op jit(solution)/shard_map/ppermute | solution.py:37
  192.2 2.1 collective-permute-start.12
  194.5 7.5 %collective-permute-done.12 = f32[3,1,65,33]{2,3,0,1:T(8,128)S(1)} collective-permute-done((f32[3,1,65,33]{2,3,0,1:T(8,128)S(1)}, f32[3,1,65,33]{2,3,0,1:T(8,128)S(1)}, u32[]{:S(2)}, u32[]{:S(2)}) %collective-permute-start.12) | collective-permute-done | bytes 25772 | tf_op jit(solution)/shard_map/ppermute | solution.py:37
  203.6 2.2 collective-permute-start.13
  205.8 6.1 %collective-permute-done.13 = f32[3,1,65,33]{2,3,0,1:T(8,128)S(1)} collective-permute-done((f32[3,1,65,33]{2,3,0,1:T(8,128)S(1)}, f32[3,1,65,33]{2,3,0,1:T(8,128)S(1)}, u32[]{:S(2)}, u32[]{:S(2)}) %collective-permute-start.13) | collective-permute-done | bytes 25772 | tf_op jit(solution)/shard_map/ppermute | solution.py:37
  214.0 7.6 %collective-permute-done.14 = f32[3,1,65,33]{2,3,0,1:T(8,128)S(1)} collective-permute-done((f32[3,1,65,33]{2,3,0,1:T(8,128)S(1)}, f32[3,1,65,33]{2,3,0,1:T(8,128)S(1)}, u32[]{:S(2)}, u32[]{:S(2)}) %collective-permute-start.14) | collective-permute-done | bytes 25772 | tf_op jit(solution)/shard_map/ppermute | solution.py:37
  225.2 5.7 %collective-permute-done.15 = f32[3,1,65,33]{2,3,0,1:T(8,128)S(1)} collective-permute-done((f32[3,1,65,33]{2,3,0,1:T(8,128)S(1)}, f32[3,1,65,33]{2,3,0,1:T(8,128)S(1)}, u32[]{:S(2)}, u32[]{:S(2)}) %collective-permute-start.15) | collective-permute-done | bytes 25772 | tf_op jit(solution)/shard_map/ppermute | solution.py:37
  (104 shorter events, 21.2 us)
Async XLA Ops:
  7.2 74.0 %all-gather.2.cloned.1.call-start = ((), (), s32[]{:S(2)}) async-start(), calls=%async_computation | async-start | bytes 5570560 | tf_op jit(solution)/shard_map/all_gather | solution.py:202
  7.9 7.9 %collective-permute-start = (f32[1,16,128]{2,1,0:T(8,128)S(1)}, f32[1,16,128]{2,1,0:T(8,128)S(1)}, u32[]{:S(2)}, u32[]{:S(2)}) collective-permute-start(f32[1,16,128]{2,1,0:T(8,128)S(1)} %get-tuple-element.72), channel_id=1, source_target_pairs={{0,16},{16,32},{32,48},{48,64},{64,80},{80,96},{96,112},{112,128},... | collective-permute-start | bytes 24584 | tf_op jit(solution)/shard_map/ppermute | solution.py:25
  13.8 9.2 %collective-permute-start.1 = (f32[1,16,128]{2,1,0:T(8,128)S(1)}, f32[1,16,128]{2,1,0:T(8,128)S(1)}, u32[]{:S(2)}, u32[]{:S(2)}) collective-permute-start(f32[1,16,128]{2,1,0:T(8,128)S(1)} %get-tuple-element.71), channel_id=1, source_target_pairs={{16,0},{32,16},{48,32},{64,48},{80,64},{96,80},{112,96},{128,112},... | collective-permute-start | bytes 24584 | tf_op jit(solution)/shard_map/ppermute | solution.py:27
  23.0 4.4 %collective-permute-start.3 = (f32[6,1,128]{2,1,0:T(1,128)S(1)}, f32[6,1,128]{2,1,0:T(1,128)S(1)}, u32[]{:S(2)}, u32[]{:S(2)}) collective-permute-start(f32[6,1,128]{2,1,0:T(1,128)S(1)} %get-tuple-element.70), channel_id=1, source_target_pairs={{1,0},{2,1},{3,2},{4,3},{5,4},{6,5},{7,6},{8,7},{9,8},{10,9},{11,1... | collective-permute-start | bytes 9224 | tf_op jit(solution)/shard_map/ppermute | solution.py:27
  25.3 7.0 %collective-permute-start.2 = (f32[6,1,128]{2,1,0:T(1,128)S(1)}, f32[6,1,128]{2,1,0:T(1,128)S(1)}, u32[]{:S(2)}, u32[]{:S(2)}) collective-permute-start(f32[6,1,128]{2,1,0:T(1,128)S(1)} %get-tuple-element.69), channel_id=1, source_target_pairs={{0,1},{1,2},{2,3},{3,4},{4,5},{5,6},{6,7},{7,8},{8,9},{9,10},{10,1... | collective-permute-start | bytes 9224 | tf_op jit(solution)/shard_map/ppermute | solution.py:25
  62.7 68.3 %collective-permute-start.4 = (f32[3,1,65,33]{2,3,0,1:T(8,128)S(1)}, f32[3,1,65,33]{2,3,0,1:T(8,128)S(1)}, u32[]{:S(2)}, u32[]{:S(2)}) collective-permute-start(f32[3,1,65,33]{2,3,0,1:T(8,128)S(1)} %slice.677), channel_id=1, source_target_pairs={{0,16},{16,32},{32,48},{48,64},{64,80},{80,96},{96,112},{112,128},... | collective-permute-start | bytes 77228 | tf_op jit(solution)/shard_map/ppermute | solution.py:37
  115.2 15.8 %collective-permute-start.5 = (f32[3,1,65,33]{2,3,0,1:T(8,128)S(1)}, f32[3,1,65,33]{2,3,0,1:T(8,128)S(1)}, u32[]{:S(2)}, u32[]{:S(2)}) collective-permute-start(f32[3,1,65,33]{2,3,0,1:T(8,128)S(1)} %slice.687), channel_id=1, source_target_pairs={{0,16},{16,32},{32,48},{48,64},{64,80},{80,96},{96,112},{112,128},... | collective-permute-start | bytes 77228 | tf_op jit(solution)/shard_map/ppermute | solution.py:37
  131.0 33.0 %copy-start = (f32[576,1,64,32]{2,3,0,1:T(8,128)S(1)}, f32[576,1,64,32]{2,3,0,1:T(8,128)}, u32[]{:S(2)}) copy-start(f32[576,1,64,32]{2,3,0,1:T(8,128)} %copy.278) | copy-start | bytes 14155780
  131.0 10.0 %collective-permute-start.6 = (f32[3,1,65,33]{2,3,0,1:T(8,128)S(1)}, f32[3,1,65,33]{2,3,0,1:T(8,128)S(1)}, u32[]{:S(2)}, u32[]{:S(2)}) collective-permute-start(f32[3,1,65,33]{2,3,0,1:T(8,128)S(1)} %get-tuple-element.8), channel_id=1, source_target_pairs={{16,0},{32,16},{48,32},{64,48},{80,64},{96,80},{112,96},{128,112},... | collective-permute-start | bytes 77228 | tf_op jit(solution)/shard_map/ppermute | solution.py:37
  146.4 7.6 %collective-permute-start.7 = (f32[3,1,65,33]{2,3,0,1:T(8,128)S(1)}, f32[3,1,65,33]{2,3,0,1:T(8,128)S(1)}, u32[]{:S(2)}, u32[]{:S(2)}) collective-permute-start(f32[3,1,65,33]{2,3,0,1:T(8,128)S(1)} %slice.705), channel_id=1, source_target_pairs={{0,16},{16,32},{32,48},{48,64},{64,80},{80,96},{96,112},{112,128},... | collective-permute-start | bytes 77228 | tf_op jit(solution)/shard_map/ppermute | solution.py:37
  154.1 9.7 %collective-permute-start.8 = (f32[3,1,65,33]{2,3,0,1:T(8,128)S(1)}, f32[3,1,65,33]{2,3,0,1:T(8,128)S(1)}, u32[]{:S(2)}, u32[]{:S(2)}) collective-permute-start(f32[3,1,65,33]{2,3,0,1:T(8,128)S(1)} %fusion.20), channel_id=1, source_target_pairs={{16,0},{32,16},{48,32},{64,48},{80,64},{96,80},{112,96},{128,112},... | collective-permute-start | bytes 77228 | tf_op jit(solution)/shard_map/ppermute | solution.py:37
  165.5 7.6 %collective-permute-start.9 = (f32[3,1,65,33]{2,3,0,1:T(8,128)S(1)}, f32[3,1,65,33]{2,3,0,1:T(8,128)S(1)}, u32[]{:S(2)}, u32[]{:S(2)}) collective-permute-start(f32[3,1,65,33]{2,3,0,1:T(8,128)S(1)} %slice.723), channel_id=1, source_target_pairs={{0,16},{16,32},{32,48},{48,64},{64,80},{80,96},{96,112},{112,128},... | collective-permute-start | bytes 77228 | tf_op jit(solution)/shard_map/ppermute | solution.py:37
  173.1 9.7 %collective-permute-start.10 = (f32[3,1,65,33]{2,3,0,1:T(8,128)S(1)}, f32[3,1,65,33]{2,3,0,1:T(8,128)S(1)}, u32[]{:S(2)}, u32[]{:S(2)}) collective-permute-start(f32[3,1,65,33]{2,3,0,1:T(8,128)S(1)} %fusion.16), channel_id=1, source_target_pairs={{16,0},{32,16},{48,32},{64,48},{80,64},{96,80},{112,96},{128,112},... | collective-permute-start | bytes 77228 | tf_op jit(solution)/shard_map/ppermute | solution.py:37
  184.5 7.6 %collective-permute-start.11 = (f32[3,1,65,33]{2,3,0,1:T(8,128)S(1)}, f32[3,1,65,33]{2,3,0,1:T(8,128)S(1)}, u32[]{:S(2)}, u32[]{:S(2)}) collective-permute-start(f32[3,1,65,33]{2,3,0,1:T(8,128)S(1)} %slice.741), channel_id=1, source_target_pairs={{0,16},{16,32},{32,48},{48,64},{64,80},{80,96},{96,112},{112,128},... | collective-permute-start | bytes 77228 | tf_op jit(solution)/shard_map/ppermute | solution.py:37
  192.2 9.8 %collective-permute-start.12 = (f32[3,1,65,33]{2,3,0,1:T(8,128)S(1)}, f32[3,1,65,33]{2,3,0,1:T(8,128)S(1)}, u32[]{:S(2)}, u32[]{:S(2)}) collective-permute-start(f32[3,1,65,33]{2,3,0,1:T(8,128)S(1)} %fusion.12), channel_id=1, source_target_pairs={{16,0},{32,16},{48,32},{64,48},{80,64},{96,80},{112,96},{128,112},... | collective-permute-start | bytes 77228 | tf_op jit(solution)/shard_map/ppermute | solution.py:37
  203.6 8.2 %collective-permute-start.13 = (f32[3,1,65,33]{2,3,0,1:T(8,128)S(1)}, f32[3,1,65,33]{2,3,0,1:T(8,128)S(1)}, u32[]{:S(2)}, u32[]{:S(2)}) collective-permute-start(f32[3,1,65,33]{2,3,0,1:T(8,128)S(1)} %slice.759), channel_id=1, source_target_pairs={{0,16},{16,32},{32,48},{48,64},{64,80},{80,96},{96,112},{112,128},... | collective-permute-start | bytes 77228 | tf_op jit(solution)/shard_map/ppermute | solution.py:37
  211.9 9.7 %collective-permute-start.14 = (f32[3,1,65,33]{2,3,0,1:T(8,128)S(1)}, f32[3,1,65,33]{2,3,0,1:T(8,128)S(1)}, u32[]{:S(2)}, u32[]{:S(2)}) collective-permute-start(f32[3,1,65,33]{2,3,0,1:T(8,128)S(1)} %fusion.8), channel_id=1, source_target_pairs={{16,0},{32,16},{48,32},{64,48},{80,64},{96,80},{112,96},{128,112},... | collective-permute-start | bytes 77228 | tf_op jit(solution)/shard_map/ppermute | solution.py:37
  223.3 7.6 %collective-permute-start.15 = (f32[3,1,65,33]{2,3,0,1:T(8,128)S(1)}, f32[3,1,65,33]{2,3,0,1:T(8,128)S(1)}, u32[]{:S(2)}, u32[]{:S(2)}) collective-permute-start(f32[3,1,65,33]{2,3,0,1:T(8,128)S(1)} %slice.777), channel_id=1, source_target_pairs={{0,16},{16,32},{32,48},{48,64},{64,80},{80,96},{96,112},{112,128},... | collective-permute-start | bytes 77228 | tf_op jit(solution)/shard_map/ppermute | solution.py:37
Sparse Core Ops, SparseCore 0:
  41.0 40.1 all-gather.1
where the time goes:
time: 241 us; the launch traced here: 238 us
  waiting for transfers between devices  92.2 us (38%)
  local copies, waits for them, and re-layouts  54.5 us (23%)
  starting transfers between devices  41.4 us (17%)
  blocking collectives  20.6 us (9%)
  between operations  14.7 us (6%)
  other arithmetic  13 us (5%)
    ppermute x12, waiting for transfers between devices, from_behind(): return lax.ppermute(value, axis, pairs)  65.7 us
    slice x1, local copies, waits for them, and re-layouts, body(): diagonal_part = scatter_nodes(stored[::25])  33.1 us
    ppermute x12, starting transfers between devices, from_behind(): return lax.ppermute(value, axis, pairs)  29.3 us
    all_gather x1, blocking collectives, body(): lax.all_gather(element_load, 'gy', axis=2, tiled=True)  20.6 us
    all_gather x1, waiting for transfers between devices, body(): lax.all_gather(outgoing, 'gy', axis=2, tiled=True)  15.2 us
    unnamed x43, local copies, waits for them, and re-layouts  15 us
    dot_general x5, other arithmetic, apply_blocks(): jnp.einsum('abxyz,bxyz->axyz', blocks, element_dofs(node_values), precisi...  9.99 us
    ppermute x2, starting transfers between devices, padded_2(): lax.ppermute(tail, axis, [(i, (i + 1) % count) for i in range(ends)])  7.89 us
  transfers between devices with their start and end apart: 17, of which 13 were waited for; matrix products, arithmetic and copies ran while one was open for 20% of the time, Pallas kernels for 0%

commit v1 on v0

v1 whole, which is shorter than its diff:
```python
import math

import jax
import jax.numpy as jnp
import numpy as np
from jax import lax
from jax.experimental import pallas as pl
from jax.experimental.pallas import tpu as pltpu
from jax.sharding import PartitionSpec as P

SWEEPS = 6
RELAX = 0.6
YOUNG_MIN = 0.001
EDGE = 1.5 - math.sqrt(2.0)
MESH = pl.DeviceIdType.MESH
GAP = 40
ROWS = 88


def corner_bits(corner_id):
    return [corner_id >> 2 & 1, corner_id >> 1 & 1, corner_id & 1]


def stiffness_table():
    poisson = 0.3
    lame_first = poisson / ((1.0 + poisson) * (1.0 - 2.0 * poisson))
    lame_shear = 1.0 / (2.0 * (1.0 + poisson))
    elastic = np.zeros((6, 6))
    elastic[:3, :3] = lame_first
    for dim_index in range(3):
        elastic[dim_index, dim_index] += 2.0 * lame_shear
        elastic[3 + dim_index, 3 + dim_index] = lame_shear
    corners = np.array([corner_bits(corner_id) for corner_id in range(8)])
    gauss_points = [0.5 - 0.5 / math.sqrt(3.0), 0.5 + 0.5 / math.sqrt(3.0)]
    matrix_sum = np.zeros((24, 24))
    for gauss_x in gauss_points:
        for gauss_y in gauss_points:
            for gauss_z in gauss_points:
                location = np.array([gauss_x, gauss_y, gauss_z])
                shape_values = np.where(corners == 1, location, 1.0 - location)
                gradients = np.zeros((8, 3))
                for dim_index in range(3):
                    slope_sign = np.where(corners[:, dim_index] == 1, 1.0, -1.0)
                    others = (
                        shape_values[:, (dim_index + 1) % 3] * shape_values[:, (dim_index + 2) % 3]
                    )
                    gradients[:, dim_index] = slope_sign * others
                strain = np.zeros((6, 24))
                for dim_index in range(3):
                    strain[dim_index, 8 * dim_index : 8 * dim_index + 8] = gradients[:, dim_index]
                for shear_index, (dim_p, dim_q) in enumerate([(0, 1), (1, 2), (0, 2)]):
                    strain[3 + shear_index, 8 * dim_p : 8 * dim_p + 8] = gradients[:, dim_q]
                    strain[3 + shear_index, 8 * dim_q : 8 * dim_q + 8] = gradients[:, dim_p]
                matrix_sum = matrix_sum + 0.125 * strain.T @ elastic @ strain
    return matrix_sum


def prolong_table():
    matrix_set = np.zeros((8, 24, 24))
    for child_id in range(8):
        child_bits = corner_bits(child_id)
        for fine_node in range(8):
            fine_bits = corner_bits(fine_node)
            for coarse_node in range(8):
                coarse_bits = corner_bits(coarse_node)
                factor = 1.0
                for dim_index in range(3):
                    position = (child_bits[dim_index] + fine_bits[dim_index]) / 2.0
                    factor = factor * (position if coarse_bits[dim_index] == 1 else 1.0 - position)
                for component in range(3):
                    matrix_set[child_id, 8 * component + fine_node, 8 * component + coarse_node] = (
                        factor
                    )
    return matrix_set


def fine_table():
    prolong = prolong_table()
    stiffness = stiffness_table()
    table = np.zeros((24, 24, 4, 4, 4))
    for outer_id in range(8):
        outer_bits = corner_bits(outer_id)
        for inner_id in range(8):
            inner_bits = corner_bits(inner_id)
            inner = prolong[inner_id].T @ stiffness @ prolong[inner_id]
            spot = tuple(2 * o + i for o, i in zip(outer_bits, inner_bits))
            table[(slice(None), slice(None)) + spot] = prolong[outer_id].T @ inner @ prolong[outer_id]
    return table


def split_16(values):
    high = jnp.asarray(values, jnp.float32).astype(jnp.bfloat16)
    low = (jnp.asarray(values, jnp.float32) - high.astype(jnp.float32)).astype(jnp.bfloat16)
    return high, low


def stencil_table():
    fine = fine_table()
    table = np.zeros((3, ROWS, 8, 4, 4, 4))
    for comp_b in range(3):
        for comp_a in range(3):
            for corner_k in range(8):
                bits_k = corner_bits(corner_k)
                for corner_l in range(8):
                    bits_l = corner_bits(corner_l)
                    step = [l - k + 1 for l, k in zip(bits_l, bits_k)]
                    row = comp_a * 27 + step[0] * 9 + step[1] * 3 + step[2]
                    block = fine[8 * comp_a + corner_k, 8 * comp_b + corner_l]
                    table[comp_b, row, corner_k] += block.transpose(2, 0, 1)
    high, low = split_16(table.reshape(3 * ROWS, 512))
    return jnp.concatenate([high, low], axis=0)


def deal_table():
    table = np.zeros((128, 128), np.float32)
    for cz in range(4):
        for elem in range(32):
            table[4 * elem + cz, 32 * cz + elem] = 1.0
    return jnp.asarray(table, jnp.bfloat16)


def spread_table():
    table = np.zeros((2, 4, 32, 2, 4, 2, 64), np.float32)
    for half in range(2):
        for cz in range(4):
            for elem in range(32):
                for bz in range(2):
                    table[half, cz, elem, bz, cz, half, elem + bz] = 1.0
    return jnp.asarray(table.reshape(256, 1024), jnp.bfloat16)


def dot(left, right):
    return jnp.dot(left, right, preferred_element_type=jnp.float32)


def turn(value, shift, axis):
    shift = shift % value.shape[axis]
    return value if shift == 0 else pltpu.roll(value, shift, axis)


def kernel(
    count_x,
    count_y,
    dens,
    pas,
    load,
    table_far,
    deal_far,
    spread_far,
    phys,
    sol,
    halo,
    units,
    loads,
    nodes,
    whole,
    last,
    stencil,
    table,
    deal,
    spread,
    wide,
    near_sem,
    halo_out,
    halo_in,
    unit_out,
    unit_in,
    load_out,
    load_in,
    node_out,
    node_in,
    whole_out,
    whole_in,
):
    at_x = lax.axis_index("gx")
    at_y = lax.axis_index("gy")

    def there(step_x, step_y):
        return (
            (at_x + step_x >= 0)
            & (at_x + step_x < count_x)
            & (at_y + step_y >= 0)
            & (at_y + step_y < count_y)
        )

    def place(step_x, step_y):
        return (at_x + step_x, at_y + step_y)

    fetches = [
        pltpu.make_async_copy(far, near, near_sem.at[index])
        for index, (far, near) in enumerate(
            [(deal_far, deal), (spread_far, spread), (table_far, table)]
        )
    ]
    for fetch in fetches:
        fetch.start()

    halo[...] = jnp.zeros_like(halo)
    units[...] = jnp.zeros_like(units)
    loads[...] = jnp.zeros_like(loads)
    nodes[...] = jnp.zeros_like(nodes)
    wide[...] = jnp.zeros_like(wide)

    barrier = pltpu.get_barrier_semaphore()
    close = [(x, y) for x in range(-2, 3) for y in range(-1, 2) if (x, y) != (0, 0)]
    heard = count_y - 1
    for step_x, step_y in close:

        @pl.when(there(step_x, step_y))
        def _(step_x=step_x, step_y=step_y):
            pl.semaphore_signal(
                barrier, inc=1, device_id=place(step_x, step_y), device_id_type=MESH
            )

        if step_x != 0:
            heard = heard + jnp.where(there(step_x, step_y), 1, 0)

    def greet(other, carry):
        @pl.when((other < at_y - 1) | (other > at_y + 1))
        def _():
            pl.semaphore_signal(barrier, inc=1, device_id=(at_x, other), device_id_type=MESH)

        return carry

    lax.fori_loop(0, count_y, greet, 0)

    for row in range(24):
        by = row // 2 % 2
        wide[row, 2 + by : 6 + by, 0:32] = load[row, 0]
    for bx in range(2):
        total = None
        for comp in range(3):
            for bz in range(2):
                row = 8 * comp + 4 * bx + bz
                term = turn(wide[row] + wide[row + 2], GAP * comp + bz, 1)
                total = term if total is None else total + term
        loads[2, 1, bx] = total

    pl.semaphore_wait(barrier, heard)

    def halo_parts(step_x, step_y):
        source_x = pl.ds(0, 4) if step_x == 0 else pl.ds(3, 1) if step_x == 1 else pl.ds(0, 1)
        target_x = pl.ds(1, 4) if step_x == 0 else pl.ds(0, 1) if step_x == 1 else pl.ds(5, 1)
        source_y = pl.ds(0, 16) if step_y == 0 else pl.ds(8, 8) if step_y == 1 else pl.ds(0, 8)
        target_y = pl.ds(8, 16) if step_y == 0 else pl.ds(0, 8) if step_y == 1 else pl.ds(24, 8)
        return dens.at[source_x, source_y], halo.at[target_x, target_y]

    def unit_parts(step_x, step_y):
        rows, target = {0: ((2, 4), 2), 1: ((4, 2), 0), -1: ((2, 1), 6)}[step_y]
        return (
            units.at[2, pl.ds(rows[0], rows[1])],
            units.at[2 - step_x, pl.ds(target, rows[1])],
        )

    def load_parts(step_x, step_y):
        return loads.at[2, 1], loads.at[2 - step_x, 1 - step_y]

    def node_parts(turn_index):
        def parts(step_x, step_y):
            return nodes.at[turn_index, 2, 1], nodes.at[turn_index, 2 - step_x, 1 - step_y]

        return parts

    def exchange(steps, parts, out_sems, in_sems):
        def copy(index, step):
            source, target = parts(*step)
            return pltpu.make_async_remote_copy(
                source,
                target,
                out_sems.at[index],
                in_sems.at[index],
                device_id=place(*step),
                device_id_type=MESH,
            )

        def send():
            for index, step in enumerate(steps):

                @pl.when(there(*step))
                def _(index=index, step=step):
                    copy(index, step).start()

        def receive():
            for index, (step_x, step_y) in enumerate(steps):

                @pl.when(there(-step_x, -step_y))
                def _(index=index, step=(step_x, step_y)):
                    copy(index, step).wait_recv()

        def finish():
            for index, step in enumerate(steps):

                @pl.when(there(*step))
                def _(index=index, step=step):
                    copy(index, step).wait_send()

        return send, receive, finish

    ring = [(x, y) for x in range(-1, 2) for y in range(-1, 2) if (x, y) != (0, 0)]
    fan = [(x, y) for x in range(-1, 3) for y in range(-1, 2) if (x, y) != (0, 0)]
    halo_send, halo_receive, halo_finish = exchange(ring, halo_parts, halo_out, halo_in)
    load_send, load_receive, load_finish = exchange(fan, load_parts, load_out, load_in)
    unit_send, unit_receive, unit_finish = exchange(fan, unit_parts, unit_out, unit_in)
    halo_send()
    load_send()
    halo[1:5, 8:24] = dens[...]

    row_at = lax.broadcasted_iota(jnp.int32, (16, 128), 0) + 16 * at_y
    lane_at = lax.broadcasted_iota(jnp.int32, (16, 128), 1)
    near_y = 2.0 - jnp.where(row_at == 0, 1.0, 0.0) - jnp.where(row_at == 16 * count_y - 1, 1.0, 0.0)
    near_z = 2.0 - jnp.where(lane_at == 0, 1.0, 0.0) - jnp.where(lane_at == 127, 1.0, 0.0)
    lane_tall = lax.broadcasted_iota(jnp.int32, (32, 128), 1)
    halo_receive()
    beside, middle = [], []
    for layer in range(6):
        cells = halo[layer]
        along_z = jnp.where(lane_tall > 0, turn(cells, 1, 1), 0.0) + jnp.where(
            lane_tall < 127, turn(cells, -1, 1), 0.0
        )
        cross = along_z + turn(cells, 1, 0) + turn(cells, -1, 0)
        beside.append((0.5 * cells + EDGE * cross)[8:24])
        if 0 < layer < 5:
            corner = turn(along_z, 1, 0) + turn(along_z, -1, 0)
            middle.append((1.5 * cells + 0.5 * cross + EDGE * corner)[8:24])
    moduli = []
    for layer in range(4):
        place_x = 4 * at_x + layer
        near_x = (
            2.0
            - jnp.where(place_x == 0, 1.0, 0.0)
            - jnp.where(place_x == 4 * count_x - 1, 1.0, 0.0)
        )
        weight = (
            1.5
            + 0.5 * (near_x + near_y + near_z)
            + EDGE * (near_x * near_y + near_x * near_z + near_y * near_z)
        )
        filtered = (middle[layer] + beside[layer] + beside[layer + 2]) / weight
        solid = jnp.where(pas[layer] == 1, 1.0, filtered)
        phys[layer] = solid
        moduli.append(YOUNG_MIN + (1.0 - YOUNG_MIN) * (solid * solid * solid))

    fetches[0].wait()
    fine = jnp.concatenate(moduli, axis=0)
    high = fine.astype(jnp.bfloat16)
    low = (fine - high.astype(jnp.float32)).astype(jnp.bfloat16)
    dealt = dot(high, deal[...]) + dot(low, deal[...])
    upper = lax.broadcasted_iota(jnp.int32, (8, 128), 0) < 4
    for pair in range(2):
        for half in range(2):
            first = dealt[32 * pair + 8 * half : 32 * pair + 8 * half + 8]
            second = dealt[32 * pair + 16 + 8 * half : 32 * pair + 16 + 8 * half + 8]
            units[2, 2 + 2 * half, 8 * pair : 8 * pair + 8] = jnp.where(
                upper, first, turn(second, 4, 0)
            )
            units[2, 3 + 2 * half, 8 * pair : 8 * pair + 8] = jnp.where(
                upper, turn(first, 4, 0), second
            )
    unit_send()

    lane = lax.broadcasted_iota(jnp.int32, (8, 128), 1)
    row = lax.broadcasted_iota(jnp.int32, (8, 128), 0)
    group_0 = lane < GAP
    group_1 = lane < 2 * GAP
    last_row = jnp.where(at_y == count_y - 1, 6, 5)
    own = (row >= 2) & (row <= last_row)
    inner = (row >= 1) & (row <= 6)

    def window(left, centre, right):
        return jnp.where(row < 3, turn(left, 4, 0), 0.0) + centre + jnp.where(
            row > 5, turn(right, 4, 0), 0.0
        )

    load_receive()
    right_side = []
    for layer in range(1, 4):
        total = None
        for bx in range(2):
            term = window(*[loads[layer - bx, side, bx] for side in range(3)])
            total = term if total is None else total + term
        right_side.append(total)

    unit_receive()
    fetches[1].wait()
    fetches[2].wait()
    blank = jnp.zeros((16, 128), jnp.float32)
    spread_high, spread_low = [], []
    for layer in range(4):
        pieces = []
        for by in range(2):
            for pair in range(4):
                spots = [2 * pair - by, 2 * pair - by + 1]
                pieces.append(
                    jnp.concatenate(
                        [units[layer, q] if 0 <= q < 7 else blank for q in spots], axis=1
                    )
                )
        both = jnp.concatenate(pieces, axis=0)
        high = both.astype(jnp.bfloat16)
        low = (both - high.astype(jnp.float32)).astype(jnp.bfloat16)
        spread_high.append(dot(high, spread[...]).astype(jnp.bfloat16))
        spread_low.append(dot(low, spread[...]).astype(jnp.bfloat16))

    def around(parts, layer):
        rows = []
        for bx in range(2):
            for by in range(2):
                for bz in range(2):
                    for cz in range(4):
                        spot = 128 * (4 * bz + cz)
                        rows.append(
                            jnp.concatenate(
                                [
                                    parts[layer - bx][
                                        16 * (4 * by + pair) : 16 * (4 * by + pair) + 16,
                                        spot : spot + 128,
                                    ]
                                    for pair in range(4)
                                ],
                                axis=1,
                            )
                        )
        return jnp.concatenate(rows, axis=0)

    wide_lane = lax.broadcasted_iota(jnp.int32, (ROWS, 128), 1)
    table_high = table[0 : 3 * ROWS]
    table_low = table[3 * ROWS : 6 * ROWS]
    for layer in range(1, 4):
        high = around(spread_high, layer)
        low = around(spread_low, layer)
        terms = dot(table_high, high) + dot(table_high, low) + dot(table_low, high)
        for spot in range(1, 7):
            tiles = []
            for comp in range(3):
                tile = terms[
                    ROWS * comp : ROWS * comp + ROWS, 128 * (spot // 2) : 128 * (spot // 2) + 128
                ]
                tiles.append(turn(tile, GAP * comp - 64 * (spot % 2), 1))
            merged = jnp.where(
                wide_lane < GAP, tiles[0], jnp.where(wide_lane < 2 * GAP, tiles[1], tiles[2])
            )
            stencil[layer - 1, pl.ds(spot, ROWS, stride=8), :] = merged

    def entry(layer, index):
        return stencil[layer - 1, 8 * index : 8 * index + 8, :]

    def pick(parts):
        return jnp.where(group_0, parts[0], jnp.where(group_1, parts[1], parts[2]))

    scale = []
    for layer in range(1, 4):
        diagonal = pick([entry(layer, 27 * comp + 13) for comp in range(3)])
        real = inner & (diagonal > 0.0)
        if layer == 3:
            real = real & (at_x < count_x - 1)
        scale.append(jnp.where(real, RELAX / jnp.where(real, diagonal, 1.0), 0.0))

    def sweep(tiles, layer):
        sums = [None, None, None]
        for step_x in range(3):
            for step_z in range(3):
                moved_z = turn(tiles[layer + step_x - 1], 1 - step_z, 1)
                for step_y in range(3):
                    moved = turn(moved_z, 1 - step_y, 0)
                    for comp in range(3):
                        index = 27 * comp + 9 * step_x + 3 * step_y + step_z
                        term = entry(layer, index) * moved
                        sums[comp] = term if sums[comp] is None else sums[comp] + term
        product = pick(
            [
                sums[0] + turn(sums[0], -GAP, 1) + turn(sums[0], -2 * GAP, 1),
                sums[1] + turn(sums[1], GAP, 1) + turn(sums[1], -GAP, 1),
                sums[2] + turn(sums[2], GAP, 1) + turn(sums[2], 2 * GAP, 1),
            ]
        )
        factor = scale[layer - 1]
        updated = tiles[layer] + factor * (right_side[layer - 1] - product)
        return jnp.where(factor > 0.0, updated, 0.0)

    def first(layer):
        return jnp.where(scale[layer - 1] > 0.0, scale[layer - 1] * right_side[layer - 1], 0.0)

    tiles = {layer: first(layer) for layer in range(1, 4)}
    mine = jnp.where(own, sweep(tiles, 2), 0.0)
    finishes = [halo_finish, load_finish, unit_finish]
    for turn_index in range(2):
        nodes[turn_index, 2, 1] = mine
        node_send, node_receive, node_finish = exchange(
            close, node_parts(turn_index), node_out.at[turn_index], node_in.at[turn_index]
        )
        finishes.append(node_finish)
        node_send()
        node_receive()
        tiles = {}
        for layer in range(5):
            left, centre, right = [nodes[turn_index, layer, side] for side in range(3)]
            tiles[layer] = centre + (
                jnp.where(row < 2, turn(left, 4, 0), 0.0)
                + jnp.where(row > 5, turn(right, 4, 0), 0.0)
            )
        after = {layer: sweep(tiles, layer) for layer in range(1, 4)}
        mine = jnp.where(own, sweep(after, 2), 0.0)

    last[...] = mine
    whole[at_y] = mine

    def whole_copy(source, other):
        return pltpu.make_async_remote_copy(
            last,
            whole.at[source],
            whole_out.at[other],
            whole_in.at[source],
            device_id=(at_x, other),
            device_id_type=MESH,
        )

    def whole_send(other, carry):
        @pl.when(other != at_y)
        def _():
            whole_copy(at_y, other).start()

        return carry

    def whole_receive(other, carry):
        @pl.when(other != at_y)
        def _():
            whole_copy(other, other).wait_recv()

        return carry

    def whole_finish(other, carry):
        @pl.when(other != at_y)
        def _():
            whole_copy(at_y, other).wait_send()

        return carry

    lax.fori_loop(0, count_y, whole_send, 0)
    for finish in finishes:
        finish()
    lax.fori_loop(0, count_y, whole_receive, 0)
    for pair in range(count_y // 2):
        rows = jnp.where(upper, turn(whole[2 * pair], -2, 0), turn(whole[2 * pair + 1], 2, 0))
        for comp in range(3):
            sol[comp, 0, 8 * pair : 8 * pair + 8, :] = turn(rows, -GAP * comp, 1)[:, 0:33]
    for comp in range(3):
        sol[comp, 0, 4 * count_y : 4 * count_y + 1, :] = turn(
            whole[count_y - 1], -GAP * comp, 1
        )[6:7, 0:33]
    lax.fori_loop(0, count_y, whole_finish, 0)


def solution(mesh):
    count_x = mesh.shape["gx"]
    count_y = mesh.shape["gy"]

    def body(density, passive, element_load):
        vmem = pl.BlockSpec(memory_space=pltpu.VMEM)
        far = pl.BlockSpec(memory_space=pl.ANY)
        dma = pltpu.SemaphoreType.DMA

        def run(*operands):
            kernel(count_x, count_y, *operands)

        return pl.pallas_call(
            run,
            out_shape=(
                jax.ShapeDtypeStruct(density.shape, jnp.float32),
                jax.ShapeDtypeStruct((3, 1, 4 * count_y + 1, 33), jnp.float32),
            ),
            in_specs=[vmem, vmem, vmem, far, far, far],
            out_specs=(vmem, vmem),
            scratch_shapes=[
                pltpu.VMEM((6, 32, 128), jnp.float32),
                pltpu.VMEM((4, 7, 16, 128), jnp.float32),
                pltpu.VMEM((4, 3, 2, 8, 128), jnp.float32),
                pltpu.VMEM((2, 5, 3, 8, 128), jnp.float32),
                pltpu.VMEM((count_y, 8, 128), jnp.float32),
                pltpu.VMEM((8, 128), jnp.float32),
                pltpu.VMEM((3, 8 * ROWS, 128), jnp.float32),
                pltpu.VMEM((6 * ROWS, 512), jnp.bfloat16),
                pltpu.VMEM((128, 128), jnp.bfloat16),
                pltpu.VMEM((256, 1024), jnp.bfloat16),
                pltpu.VMEM((24, 8, 128), jnp.float32),
                dma((3,)),
                dma((8,)),
                dma((8,)),
                dma((11,)),
                dma((11,)),
                dma((11,)),
                dma((11,)),
                dma((2, 14)),
                dma((2, 14)),
                dma((count_y,)),
                dma((count_y,)),
            ],
            compiler_params=pltpu.CompilerParams(collective_id=0, has_side_effects=True),
        )(density, passive, element_load, stencil_table(), deal_table(), spread_table())

    return jax.shard_map(
        body,
        mesh=mesh,
        in_specs=(P("gx", "gy", None), P("gx", "gy", None), P(None, "gx", "gy", None)),
        out_specs=(P("gx", "gy", None), P(None, "gx", None, None)),
        check_vma=False,
    )
```

time: 241 us -> 39.3 us (0.16)
  the two profiles are of different devices: /device:TPU:102 before, /device:TPU:97 now
where the time goes in v1:
time: 39.3 us; the launch traced here: 39.1 us
  Pallas kernels  36.3 us (92%)
  local copies, waits for them, and re-layouts  2.25 us (6%)
  between operations  0.65 us (2%)
    pallas_call x1, Pallas kernels, body(): pl.pallas_call(run, out_shape=(jax.ShapeDtypeStruct(density.shape, jnp.fl...  36.3 us
    pallas_call x1, local copies, waits for them, and re-layouts, body(): pl.pallas_call(run, out_shape=(jax.ShapeDtypeStruct(density.shape, jnp.fl...  1.63 us

profile of v1, /device:TPU:97, one launch (start us, length us, event | category | flops | bytes accessed | tf_op | source)
XLA Modules:
  0.0 39.1 jit_solution(12031678260818435907)
XLA Ops:
  0.6 36.3 %shard_map.86 = (f32[4,16,128]{2,1,0:T(8,128)}, f32[3,1,65,33]{3,2,1,0:T(8,128)}) custom-call(f32[4,16,128]{2,1,0:T(8,128)} %operands_0_.1, s32[4,16,128]{2,1,0:T(8,128)} %operands_1_.1, f32[24,1,4,32]{3,2,1,0:T(4,128)} %operands_2_.1, bf16[528,512]{1,0:T(8,128)(2,1)} %constant.16.operands_3_, bf16[128,128]{1,0:T(8,128)(2,1)} %constant.7.clone.operands_4_, ...), custom_call_target="tpu_custom_call" | custom-call | tf_op jit(solution)/shard_map/pallas_call | solution.py:565
  36.9 0.0 copy-start
  36.9 1.6 %copy.9 = f32[3,1,65,33]{2,1,3,0:T(1,128)} copy(f32[3,1,65,33]{3,2,1,0:T(8,128)} %get-tuple-element.3) | data formatting | bytes 51480 | tf_op jit(solution)/shard_map/pallas_call | solution.py:565
  38.5 0.0 copy-done
  38.5 0.6 %copy.11 = f32[4,16,128]{2,1,0:T(8,128)} copy(f32[4,16,128]{2,1,0:T(8,128)S(1)} %copy-done) | data formatting | bytes 65536
Async XLA Ops:
  36.9 1.6 %copy-start = (f32[4,16,128]{2,1,0:T(8,128)S(1)}, f32[4,16,128]{2,1,0:T(8,128)}, u32[]{:S(2)}) copy-start(f32[4,16,128]{2,1,0:T(8,128)} %get-tuple-element.6) | copy-start | bytes 98308

commit v2 on v1

v2 whole, which is shorter than its diff:
```python
import math

import jax
import jax.numpy as jnp
import numpy as np
from jax import lax
from jax.experimental import pallas as pl
from jax.experimental.pallas import tpu as pltpu
from jax.sharding import PartitionSpec as P

SWEEPS = 6
RELAX = 0.6
YOUNG_MIN = 0.001
EDGE = 1.5 - math.sqrt(2.0)
MESH = pl.DeviceIdType.MESH
GAP = 40
ROWS = 88
FULL = 272
CENTRE = 32


def corner_bits(corner_id):
    return [corner_id >> 2 & 1, corner_id >> 1 & 1, corner_id & 1]


def stiffness_table():
    poisson = 0.3
    lame_first = poisson / ((1.0 + poisson) * (1.0 - 2.0 * poisson))
    lame_shear = 1.0 / (2.0 * (1.0 + poisson))
    elastic = np.zeros((6, 6))
    elastic[:3, :3] = lame_first
    for dim_index in range(3):
        elastic[dim_index, dim_index] += 2.0 * lame_shear
        elastic[3 + dim_index, 3 + dim_index] = lame_shear
    corners = np.array([corner_bits(corner_id) for corner_id in range(8)])
    gauss_points = [0.5 - 0.5 / math.sqrt(3.0), 0.5 + 0.5 / math.sqrt(3.0)]
    matrix_sum = np.zeros((24, 24))
    for gauss_x in gauss_points:
        for gauss_y in gauss_points:
            for gauss_z in gauss_points:
                location = np.array([gauss_x, gauss_y, gauss_z])
                shape_values = np.where(corners == 1, location, 1.0 - location)
                gradients = np.zeros((8, 3))
                for dim_index in range(3):
                    slope_sign = np.where(corners[:, dim_index] == 1, 1.0, -1.0)
                    others = (
                        shape_values[:, (dim_index + 1) % 3] * shape_values[:, (dim_index + 2) % 3]
                    )
                    gradients[:, dim_index] = slope_sign * others
                strain = np.zeros((6, 24))
                for dim_index in range(3):
                    strain[dim_index, 8 * dim_index : 8 * dim_index + 8] = gradients[:, dim_index]
                for shear_index, (dim_p, dim_q) in enumerate([(0, 1), (1, 2), (0, 2)]):
                    strain[3 + shear_index, 8 * dim_p : 8 * dim_p + 8] = gradients[:, dim_q]
                    strain[3 + shear_index, 8 * dim_q : 8 * dim_q + 8] = gradients[:, dim_p]
                matrix_sum = matrix_sum + 0.125 * strain.T @ elastic @ strain
    return matrix_sum


def prolong_table():
    matrix_set = np.zeros((8, 24, 24))
    for child_id in range(8):
        child_bits = corner_bits(child_id)
        for fine_node in range(8):
            fine_bits = corner_bits(fine_node)
            for coarse_node in range(8):
                coarse_bits = corner_bits(coarse_node)
                factor = 1.0
                for dim_index in range(3):
                    position = (child_bits[dim_index] + fine_bits[dim_index]) / 2.0
                    factor = factor * (position if coarse_bits[dim_index] == 1 else 1.0 - position)
                for component in range(3):
                    matrix_set[child_id, 8 * component + fine_node, 8 * component + coarse_node] = (
                        factor
                    )
    return matrix_set


def fine_table():
    prolong = prolong_table()
    stiffness = stiffness_table()
    table = np.zeros((24, 24, 4, 4, 4))
    for outer_id in range(8):
        outer_bits = corner_bits(outer_id)
        for inner_id in range(8):
            inner_bits = corner_bits(inner_id)
            inner = prolong[inner_id].T @ stiffness @ prolong[inner_id]
            spot = tuple(2 * o + i for o, i in zip(outer_bits, inner_bits))
            table[(slice(None), slice(None)) + spot] = prolong[outer_id].T @ inner @ prolong[outer_id]
    return table


def split_16(values):
    high = jnp.asarray(values, jnp.float32).astype(jnp.bfloat16)
    low = (jnp.asarray(values, jnp.float32) - high.astype(jnp.float32)).astype(jnp.bfloat16)
    return high, low


def stencil_tables():
    fine = fine_table()
    table = np.zeros((3, ROWS, 8, 4, 4, 4))
    for comp_b in range(3):
        for comp_a in range(3):
            for corner_k in range(8):
                bits_k = corner_bits(corner_k)
                for corner_l in range(8):
                    bits_l = corner_bits(corner_l)
                    step = [l - k + 1 for l, k in zip(bits_l, bits_k)]
                    row = comp_a * 27 + step[0] * 9 + step[1] * 3 + step[2]
                    block = fine[8 * comp_a + corner_k, 8 * comp_b + corner_l]
                    table[comp_b, row, corner_k] += block.transpose(2, 0, 1)
    full = np.zeros((FULL, 512))
    full[: 3 * ROWS] = table.reshape(3 * ROWS, 512)
    centre = np.zeros((CENTRE, 512))
    for comp in range(3):
        centre[8 * comp : 8 * comp + 8] = table[comp, 27 * comp + 13].reshape(1, 512)
    return [jnp.concatenate(split_16(part), axis=0) for part in (full, centre)]


def deal_table():
    table = np.zeros((128, 128), np.float32)
    for cz in range(4):
        for elem in range(32):
            table[4 * elem + cz, 32 * cz + elem] = 1.0
    return jnp.asarray(table, jnp.bfloat16)


def spread_table():
    table = np.zeros((2, 4, 32, 2, 4, 2, 64), np.float32)
    for half in range(2):
        for cz in range(4):
            for elem in range(32):
                for bz in range(2):
                    table[half, cz, elem, bz, cz, half, elem + bz] = 1.0
    return jnp.asarray(table.reshape(256, 1024), jnp.bfloat16)


def dot(left, right):
    return jnp.dot(left, right, preferred_element_type=jnp.float32)


def turn(value, shift, axis):
    shift = shift % value.shape[axis]
    return value if shift == 0 else pltpu.roll(value, shift, axis)


def kernel(
    count_x,
    count_y,
    dens_far,
    pas_far,
    load_far,
    full_far,
    centre_far,
    deal_far,
    spread_far,
    phys_far,
    sol_far,
    phys,
    sol,
    halo,
    pas,
    load,
    units,
    loads,
    nodes,
    whole,
    last,
    stencil,
    full,
    centre,
    deal,
    spread,
    wide,
    near_sem,
    halo_out,
    halo_in,
    unit_out,
    unit_in,
    load_out,
    load_in,
    node_out,
    node_in,
    whole_sem,
):
    at_x = lax.axis_index("gx")
    at_y = lax.axis_index("gy")
    plane = at_x // 2
    half_x = at_x % 2
    planes = count_x // 2

    def beside_y(step_y):
        return lax.rem(at_y + (step_y + count_y), count_y)

    def guarded(condition, work):
        if condition is None:
            work()
        else:
            pl.when(condition)(work)

    def wait(ref, sem):
        pltpu.make_async_copy(ref, ref, sem).wait()

    def remote(source, target, out_sem, in_sem, to_x, to_y):
        return pltpu.make_async_remote_copy(
            source, target, out_sem, in_sem, device_id=(to_x, to_y), device_id_type=MESH
        )

    fetches = [
        pltpu.make_async_copy(far, near, near_sem.at[index])
        for index, (far, near) in enumerate(
            [
                (dens_far, halo.at[pl.ds(1, 4), pl.ds(8, 16)]),
                (pas_far, pas),
                (load_far, load),
                (deal_far, deal),
                (spread_far, spread),
                (full_far, full),
                (centre_far, centre),
            ]
        )
    ]
    for fetch in fetches:
        fetch.start()

    barrier = pltpu.get_barrier_semaphore()

    def greet(to_x, steps):
        for step in steps:
            pl.semaphore_signal(
                barrier, inc=1, device_id=(to_x, beside_y(step)), device_id_type=MESH
            )

    above = plane < planes - 1
    below = plane > 0
    greet(at_x, range(1, count_y))
    greet(2 * plane + 1 - half_x, (-1, 0, 1))
    for there, to in ((below, 2 * plane - 2), (above, 2 * plane + 2)):
        for side in range(2):
            guarded(there, lambda to=to, side=side: greet(to + side, (-1, 0, 1)))
    heard = count_y + 2 + jnp.where(below, 6, 0) + jnp.where(above, 6, 0)
    fetches[0].wait()
    pl.semaphore_wait(barrier, heard)

    before = at_x > 0
    after = at_x < count_x - 1
    source_y = {0: (8, 16), 1: (16, 8), -1: (8, 8)}
    target_y = {0: 8, 1: 0, -1: 24}

    def halo_send(step_x):
        source_x, target_x, deep = {0: (1, 1, 4), 1: (4, 0, 1), -1: (1, 5, 1)}[step_x]
        for step_y in (0, 1, -1):
            if step_x == 0 and step_y == 0:
                continue
            start, size = source_y[step_y]
            remote(
                halo.at[pl.ds(source_x, deep), pl.ds(start, size)],
                halo.at[pl.ds(target_x, deep), pl.ds(target_y[step_y], size)],
                halo_out.at[step_x + 1],
                halo_in.at[step_x + 1],
                at_x + step_x,
                beside_y(step_y),
            ).start()

    guarded(before, lambda: halo_send(-1))
    guarded(after, lambda: halo_send(1))
    halo_send(0)

    mine = 2 + half_x
    wide[...] = jnp.zeros_like(wide)
    fetches[2].wait()
    for row in range(24):
        by = row // 2 % 2
        wide[row, 2 + by : 6 + by, 0:32] = load[row, 0]
    for bx in range(2):
        total = None
        for comp in range(3):
            for bz in range(2):
                row = 8 * comp + 4 * bx + bz
                term = turn(wide[row] + wide[row + 2], GAP * comp + bz, 1)
                total = term if total is None else total + term
        loads[mine, 1, bx] = total

    targets = [
        (2 * plane + 2, half_x, 2 + half_x, 2, above),
        (2 * plane + 3, half_x, 2 + half_x, 3, above),
        (2 * plane - 2, 4, 4, 4, below & (half_x == 0)),
        (2 * plane - 1, 4, 4, 5, below & (half_x == 0)),
        (2 * plane + 1 - half_x, mine, 1, 1, None),
        (at_x, mine, 0, 0, None),
    ]

    def load_send(to_x, slot, in_index, out_index):
        for step_y in (0, 1, -1):
            if out_index == 0 and step_y == 0:
                continue
            remote(
                loads.at[mine, 1],
                loads.at[slot, 1 - step_y],
                load_out.at[out_index],
                load_in.at[in_index],
                to_x,
                beside_y(step_y),
            ).start()

    def unit_send(to_x, slot, in_index, out_index):
        for step_y in (0, 1, -1):
            if out_index == 0 and step_y == 0:
                continue
            start, target, size = {0: (2, 2, 4), 1: (4, 0, 2), -1: (2, 6, 1)}[step_y]
            remote(
                units.at[mine, pl.ds(start, size)],
                units.at[slot, pl.ds(target, size)],
                unit_out.at[out_index],
                unit_in.at[in_index],
                to_x,
                beside_y(step_y),
            ).start()

    for target in targets:
        guarded(target[4], lambda target=target: load_send(*target[:4]))

    row_at = lax.broadcasted_iota(jnp.int32, (16, 128), 0) + 16 * at_y
    lane_at = lax.broadcasted_iota(jnp.int32, (16, 128), 1)
    near_y = 2.0 - jnp.where(row_at == 0, 1.0, 0.0) - jnp.where(row_at == 16 * count_y - 1, 1.0, 0.0)
    near_z = 2.0 - jnp.where(lane_at == 0, 1.0, 0.0) - jnp.where(lane_at == 127, 1.0, 0.0)
    weights = []
    for layer in range(4):
        place_x = 4 * at_x + layer
        near_x = (
            2.0
            - jnp.where(place_x == 0, 1.0, 0.0)
            - jnp.where(place_x == 4 * count_x - 1, 1.0, 0.0)
        )
        weights.append(
            1.5
            + 0.5 * (near_x + near_y + near_z)
            + EDGE * (near_x * near_y + near_x * near_z + near_y * near_z)
        )
    lane_tall = lax.broadcasted_iota(jnp.int32, (32, 128), 1)
    row_tall = lax.broadcasted_iota(jnp.int32, (32, 128), 0) + (16 * at_y - 8)
    in_grid = (row_tall >= 0) & (row_tall < 16 * count_y)
    fetches[1].wait()
    fetches[3].wait()
    wait(halo.at[pl.ds(1, 4), pl.ds(0, 16)], halo_in.at[1])
    guarded(before, lambda: wait(halo.at[0], halo_in.at[2]))
    guarded(after, lambda: wait(halo.at[5], halo_in.at[0]))
    beside, middle = [], []
    for layer in range(6):
        inside = in_grid
        if layer == 0:
            inside = inside & before
        if layer == 5:
            inside = inside & after
        cells = jnp.where(inside, halo[layer], 0.0)
        along_z = jnp.where(lane_tall > 0, turn(cells, 1, 1), 0.0) + jnp.where(
            lane_tall < 127, turn(cells, -1, 1), 0.0
        )
        cross = along_z + turn(cells, 1, 0) + turn(cells, -1, 0)
        beside.append((0.5 * cells + EDGE * cross)[8:24])
        if 0 < layer < 5:
            corner = turn(along_z, 1, 0) + turn(along_z, -1, 0)
            middle.append((1.5 * cells + 0.5 * cross + EDGE * corner)[8:24])
    moduli = []
    for layer in range(4):
        filtered = (middle[layer] + beside[layer] + beside[layer + 2]) / weights[layer]
        solid = jnp.where(pas[layer] == 1, 1.0, filtered)
        phys[layer] = solid
        moduli.append(YOUNG_MIN + (1.0 - YOUNG_MIN) * (solid * solid * solid))

    fine = jnp.concatenate(moduli, axis=0)
    high = fine.astype(jnp.bfloat16)
    low = (fine - high.astype(jnp.float32)).astype(jnp.bfloat16)
    dealt = dot(jnp.concatenate([high, low], axis=0), deal[...])
    dealt = dealt[0:64] + dealt[64:128]
    upper = lax.broadcasted_iota(jnp.int32, (8, 128), 0) < 4
    for pair in range(2):
        for half in range(2):
            first = dealt[32 * pair + 8 * half : 32 * pair + 8 * half + 8]
            second = dealt[32 * pair + 16 + 8 * half : 32 * pair + 16 + 8 * half + 8]
            units[mine, 2 + 2 * half, 8 * pair : 8 * pair + 8] = jnp.where(
                upper, first, turn(second, 4, 0)
            )
            units[mine, 3 + 2 * half, 8 * pair : 8 * pair + 8] = jnp.where(
                upper, turn(first, 4, 0), second
            )
    for target in targets:
        guarded(target[4], lambda target=target: unit_send(*target[:4]))
    phys_copy = pltpu.make_async_copy(phys, phys_far, near_sem.at[7])
    phys_copy.start()

    lane = lax.broadcasted_iota(jnp.int32, (8, 128), 1)
    row = lax.broadcasted_iota(jnp.int32, (8, 128), 0)
    groups = [lane < GAP, (lane >= GAP) & (lane < 2 * GAP), lane >= 2 * GAP]
    last_row = jnp.where(at_y == count_y - 1, 6, 5)
    own = (row >= 2) & (row <= last_row)
    inner = (row >= 1) & (row <= 6)
    has_left = at_y > 0
    has_right = at_y < count_y - 1
    has_layer = [below, below, None, None, above, above]

    def kept(value, layer):
        return value if has_layer[layer] is None else jnp.where(has_layer[layer], value, 0.0)

    from_left = (row < 3) & has_left
    from_right = (row > 5) & has_right
    wait(loads.at[2, pl.ds(0, 2)], load_in.at[0])
    wait(loads.at[3], load_in.at[1])
    guarded(below, lambda: wait(loads.at[0], load_in.at[2]))
    guarded(below, lambda: wait(loads.at[1], load_in.at[3]))
    guarded(above, lambda: wait(loads.at[4], load_in.at[4]))
    right_side = []
    for layer in range(1, 5):
        total = None
        for bx in range(2):
            left, inside, right = [loads[layer - bx, side, bx] for side in range(3)]
            term = kept(
                jnp.where(from_left, turn(left, 4, 0), 0.0)
                + inside
                + jnp.where(from_right, turn(right, 4, 0), 0.0),
                layer - bx,
            )
            total = term if total is None else total + term
        right_side.append(total)

    def unit(layer, spot):
        value = units[layer, spot]
        if spot < 2:
            value = jnp.where(has_left, value, 0.0)
        if spot == 6:
            value = jnp.where(has_right, value, 0.0)
        return kept(value, layer)

    def around(layer):
        found = [unit(layer, spot) for spot in range(7)]
        pieces = []
        for by in range(2):
            for pair in range(3):
                spot = 2 * pair + 1 - by
                pieces.append(jnp.concatenate([found[spot], found[spot + 1]], axis=1))
        both = jnp.concatenate(pieces, axis=0)
        high = both.astype(jnp.bfloat16)
        low = (both - high.astype(jnp.float32)).astype(jnp.bfloat16)
        moved = dot(jnp.concatenate([high, low], axis=0), spread[...]).astype(jnp.bfloat16)
        results = []
        for part in range(2):
            rows = []
            for by in range(2):
                for bz in range(2):
                    for cz in range(4):
                        spot = 128 * (4 * bz + cz)
                        start = 96 * part + 48 * by
                        rows.append(
                            jnp.concatenate(
                                [
                                    moved[start + 16 * pair : start + 16 * pair + 16][
                                        :, spot : spot + 128
                                    ]
                                    for pair in range(3)
                                ],
                                axis=1,
                            )
                        )
            results.append(jnp.concatenate(rows, axis=0))
        return results

    def terms(table, bx, parts):
        count = table.shape[0] // 2
        both = dot(table[:, 256 * bx : 256 * bx + 256], parts[0])
        return (
            both[0:count]
            + both[count:]
            + dot(table[0:count, 256 * bx : 256 * bx + 256], parts[1])
        )

    wide_lane = lax.broadcasted_iota(jnp.int32, (ROWS, 128), 1)

    def build(layer, total):
        for spot in range(6):
            tiles = []
            for comp in range(3):
                tile = total[
                    ROWS * comp : ROWS * comp + ROWS, 128 * (spot // 2) : 128 * (spot // 2) + 128
                ]
                tiles.append(turn(tile, GAP * comp - 64 * (spot % 2), 1))
            merged = jnp.where(
                wide_lane < GAP, tiles[0], jnp.where(wide_lane < 2 * GAP, tiles[1], tiles[2])
            )
            stencil[layer - 1, pl.ds(spot + 1, ROWS, stride=8), :] = merged

    def scale_of(layer):
        total = terms(centre, 0, parts[layer]) + terms(centre, 1, parts[layer - 1])
        diagonal = jnp.zeros((8, 128), jnp.float32)
        for spot in range(6):
            for comp in range(3):
                tile = total[8 * comp : 8 * comp + 8, 128 * (spot // 2) : 128 * (spot // 2) + 128]
                tile = turn(tile, GAP * comp - 64 * (spot % 2), 1)
                diagonal = jnp.where((row == spot + 1) & groups[comp], tile, diagonal)
        real = inner & (diagonal > 0.0)
        if layer == 4:
            real = real & above
        return jnp.where(real, RELAX / jnp.where(real, diagonal, 1.0), 0.0)

    fetches[4].wait()
    fetches[5].wait()
    fetches[6].wait()
    parts = [None] * 5
    scale = [None] * 5
    wait(units.at[2, pl.ds(0, 3)], unit_in.at[0])
    wait(units.at[3], unit_in.at[1])
    parts[2] = around(2)
    parts[3] = around(3)
    build(3, terms(full, 0, parts[3]) + terms(full, 1, parts[2]))
    scale[3] = scale_of(3)
    guarded(below, lambda: wait(units.at[1], unit_in.at[3]))
    parts[1] = around(1)
    build(2, terms(full, 0, parts[2]) + terms(full, 1, parts[1]))
    scale[2] = scale_of(2)
    guarded(below, lambda: wait(units.at[0], unit_in.at[2]))
    parts[0] = around(0)
    scale[1] = scale_of(1)
    guarded(above, lambda: wait(units.at[4], unit_in.at[4]))
    parts[4] = around(4)
    scale[4] = scale_of(4)

    def entry(layer, index):
        return stencil[layer - 1, 8 * index : 8 * index + 8, :]

    def sweep(tiles, layer):
        sums = [None, None, None]
        for step_x in range(3):
            for step_z in range(3):
                moved_z = turn(tiles[layer + step_x - 1], 1 - step_z, 1)
                for step_y in range(3):
                    moved = turn(moved_z, 1 - step_y, 0)
                    for comp in range(3):
                        index = 27 * comp + 9 * step_x + 3 * step_y + step_z
                        term = entry(layer, index) * moved
                        sums[comp] = term if sums[comp] is None else sums[comp] + term
        product = jnp.where(
            groups[0],
            sums[0] + turn(sums[0], -GAP, 1) + turn(sums[0], -2 * GAP, 1),
            jnp.where(
                groups[1],
                sums[1] + turn(sums[1], GAP, 1) + turn(sums[1], -GAP, 1),
                sums[2] + turn(sums[2], GAP, 1) + turn(sums[2], 2 * GAP, 1),
            ),
        )
        factor = scale[layer]
        updated = tiles[layer] + factor * (right_side[layer - 1] - product)
        return jnp.where(factor > 0.0, updated, 0.0)

    def first(layer):
        return jnp.where(scale[layer] > 0.0, scale[layer] * right_side[layer - 1], 0.0)

    tiles = {layer: first(layer) for layer in range(1, 5)}
    pair_now = [jnp.where(own, sweep(tiles, layer), 0.0) for layer in (2, 3)]
    left_rows = (row < 2) & has_left
    right_rows = (row > 5) & has_right

    def node_send(turn_index, step_z):
        for step_y in (1, -1, 0):
            if step_z == 0 and step_y == 0:
                continue
            remote(
                nodes.at[turn_index, 1, pl.ds(2, 2)],
                nodes.at[turn_index, 1 - step_y, pl.ds(2 - 2 * step_z, 2)],
                node_out.at[turn_index, step_z + 1],
                node_in.at[turn_index, step_z + 1],
                at_x + 2 * step_z,
                beside_y(step_y),
            ).start()

    def node_wait(turn_index, sems, flip):
        up, down = (above, below) if flip else (below, above)
        wait(nodes.at[turn_index, 0, pl.ds(0, 4)], sems.at[turn_index, 1])
        guarded(up, lambda: wait(nodes.at[turn_index, 0], sems.at[turn_index, 2]))
        guarded(down, lambda: wait(nodes.at[turn_index, 0], sems.at[turn_index, 0]))

    for turn_index in range(2):
        nodes[turn_index, 1, 2] = pair_now[0]
        nodes[turn_index, 1, 3] = pair_now[1]
        guarded(above, lambda: node_send(turn_index, 1))
        guarded(below, lambda: node_send(turn_index, -1))
        node_send(turn_index, 0)
        if turn_index == 0:
            for layer in (1, 4):
                build(
                    layer,
                    terms(full, 0, parts[layer]) + terms(full, 1, parts[layer - 1]),
                )
        node_wait(turn_index, node_in, False)
        tiles = {}
        for layer in range(6):
            left, inside, right = [nodes[turn_index, side, layer] for side in range(3)]
            tiles[layer] = kept(
                jnp.where(
                    left_rows,
                    turn(left, 4, 0),
                    jnp.where(right_rows, turn(right, 4, 0), inside),
                ),
                layer,
            )
        later = {layer: sweep(tiles, layer) for layer in range(1, 5)}
        if turn_index == 0:
            pair_now = [jnp.where(own, sweep(later, layer), 0.0) for layer in (2, 3)]

    final = jnp.where(half_x == 0, sweep(later, 2), sweep(later, 3))
    final = jnp.where(own, final, 0.0)
    last[...] = final
    whole[at_y] = final
    for step in range(1, count_y):
        remote(last, whole.at[at_y], whole_sem.at[0], whole_sem.at[1], at_x, beside_y(step)).start()

    wait(halo.at[pl.ds(1, 4), pl.ds(0, 16)], halo_out.at[1])
    guarded(after, lambda: wait(halo.at[0], halo_out.at[2]))
    guarded(before, lambda: wait(halo.at[5], halo_out.at[0]))
    for to_x, slot, in_index, out_index, there in targets:
        some = pl.ds(0, 2) if out_index == 0 else pl.ds(0, 3)
        guarded(there, lambda: wait(loads.at[2, some], load_out.at[out_index]))
        some = pl.ds(0, 3) if out_index == 0 else pl.ds(0, 7)
        guarded(there, lambda: wait(units.at[2, some], unit_out.at[out_index]))
    for turn_index in range(2):
        node_wait(turn_index, node_out, True)
    phys_copy.wait()

    wait(whole.at[pl.ds(0, count_y - 1)], whole_sem.at[1])
    columns = []
    for pair in range(count_y // 2):
        columns.append(
            jnp.where(upper, turn(whole[2 * pair], -2, 0), turn(whole[2 * pair + 1], 2, 0))
        )
    columns.append(turn(whole[count_y - 1], -6, 0))
    columns.append(jnp.zeros((128 - 8 * len(columns), 128), jnp.float32))
    across = jnp.concatenate(columns, axis=0).T
    for comp in range(3):
        sol[comp, :, 0, :] = across[GAP * comp : GAP * comp + 33, 0 : 4 * count_y + 1]
    sol_copy = pltpu.make_async_copy(sol, sol_far, near_sem.at[8])
    sol_copy.start()
    wait(whole.at[pl.ds(0, count_y - 1)], whole_sem.at[0])
    sol_copy.wait()


def solution(mesh):
    count_x = mesh.shape["gx"]
    count_y = mesh.shape["gy"]

    def body(density, passive, element_load):
        far = pl.BlockSpec(memory_space=pl.ANY)
        dma = pltpu.SemaphoreType.DMA
        across_shape = (3, 33, 1, 4 * count_y + 1)

        def run(*refs):
            kernel(count_x, count_y, *refs)

        operands = [density, passive, element_load]
        operands += [*stencil_tables(), deal_table(), spread_table()]

        physical, across = pl.pallas_call(
            run,
            out_shape=(
                jax.ShapeDtypeStruct(density.shape, jnp.float32),
                jax.ShapeDtypeStruct(across_shape, jnp.float32),
            ),
            in_specs=[far] * 7,
            out_specs=(far, far),
            scratch_shapes=[
                pltpu.VMEM(density.shape, jnp.float32),
                pltpu.VMEM(across_shape, jnp.float32),
                pltpu.VMEM((6, 32, 128), jnp.float32),
                pltpu.VMEM(passive.shape, jnp.int32),
                pltpu.VMEM(element_load.shape, jnp.float32),
                pltpu.VMEM((5, 7, 16, 128), jnp.float32),
                pltpu.VMEM((5, 3, 2, 8, 128), jnp.float32),
                pltpu.VMEM((2, 3, 6, 8, 128), jnp.float32),
                pltpu.VMEM((count_y, 8, 128), jnp.float32),
                pltpu.VMEM((8, 128), jnp.float32),
                pltpu.VMEM((4, 8 * ROWS, 128), jnp.float32),
                pltpu.VMEM((2 * FULL, 512), jnp.bfloat16),
                pltpu.VMEM((2 * CENTRE, 512), jnp.bfloat16),
                pltpu.VMEM((128, 128), jnp.bfloat16),
                pltpu.VMEM((256, 1024), jnp.bfloat16),
                pltpu.VMEM((24, 8, 128), jnp.float32),
                dma((9,)),
                dma((3,)),
                dma((3,)),
                dma((6,)),
                dma((5,)),
                dma((6,)),
                dma((5,)),
                dma((2, 3)),
                dma((2, 3)),
                dma((2,)),
            ],
            compiler_params=pltpu.CompilerParams(collective_id=0, has_side_effects=True, vmem_limit_bytes=16 * 2**20),
        )(*[pltpu.with_memory_space_constraint(operand, pltpu.HBM) for operand in operands])
        return physical, across.transpose(0, 2, 3, 1)

    return jax.shard_map(
        body,
        mesh=mesh,
        in_specs=(P("gx", "gy", None), P("gx", "gy", None), P(None, "gx", "gy", None)),
        out_specs=(P("gx", "gy", None), P(None, "gx", None, None)),
        check_vma=False,
    )
```

time: 39.3 us -> 37.6 us (0.957)
  the two profiles are of different devices: /device:TPU:97 before, /device:TPU:65 now
where the time goes in v2:
time: 37.6 us; the launch traced here: 37.5 us
  Pallas kernels  35.6 us (95%)
  local copies, waits for them, and re-layouts  1.24 us (3%)
  between operations  0.64 us (2%)
    pallas_call x1, Pallas kernels, body(): pl.pallas_call(run, out_shape=(jax.ShapeDtypeStruct(density.shape, jnp.fl...  35.6 us
    unnamed x2, local copies, waits for them, and re-layouts  1.24 us

profile of v2, /device:TPU:65, one launch (start us, length us, event | category | flops | bytes accessed | tf_op | source)
XLA Modules:
  0.0 37.5 jit_solution(16458345239140489304)
XLA Ops:
  0.6 35.6 %shard_map.104 = (f32[4,16,128]{2,1,0:T(8,128)S(1)}, f32[3,33,1,65]{3,2,1,0:T(1,128)S(1)}) custom-call(f32[4,16,128]{2,1,0:T(8,128)} %refs_0_.1, s32[4,16,128]{2,1,0:T(8,128)} %refs_1_.1, f32[24,1,4,32]{3,2,1,0:T(4,128)} %refs_2_.1, bf16[544,512]{1,0:T(8,128)(2,1)} %constant.19.refs_3_, bf16[64,512]{1,0:T(8,128)(2,1)} %constant.24.refs_4_, ...), custom_call_target="tpu_custom_call" | custom-call | tf_op jit(solution)/shard_map/pallas_call | solution.py:659
  36.2 0.6 %copy.13 = f32[4,16,128]{2,1,0:T(8,128)} copy(f32[4,16,128]{2,1,0:T(8,128)S(1)} %get-tuple-element.8) | data formatting | bytes 65536
  36.8 0.6 %copy.14 = f32[3,1,65,33]{2,1,3,0:T(1,128)} copy(f32[3,1,65,33]{2,1,3,0:T(1,128)S(1)} %bitcast.1) | data formatting | bytes 51480

commit v3 on v2

--- a/solution.py
+++ b/solution.py
@@ -154,8 +154,6 @@
     centre_far,
     deal_far,
     spread_far,
-    phys_far,
-    sol_far,
     phys,
     sol,
     halo,
@@ -220,8 +218,7 @@
             ]
         )
     ]
-    for fetch in fetches:
-        fetch.start()
+    fetches[0].start()
 
     barrier = pltpu.get_barrier_semaphore()
 
@@ -233,11 +230,17 @@
 
     above = plane < planes - 1
     below = plane > 0
-    greet(at_x, range(1, count_y))
-    greet(2 * plane + 1 - half_x, (-1, 0, 1))
     for there, to in ((below, 2 * plane - 2), (above, 2 * plane + 2)):
         for side in range(2):
-            guarded(there, lambda to=to, side=side: greet(to + side, (-1, 0, 1)))
+            guarded(there, lambda to=to, side=side: greet(to + side, (-1, 1, 0)))
+    greet(2 * plane + 1 - half_x, (-1, 1, 0))
+    far_first = sorted(
+        range(1, count_y),
+        key=lambda step: -(min(step // 2 % 4, 4 - step // 2 % 4) + step // 8 % 2),
+    )
+    greet(at_x, far_first)
+    for fetch in fetches[1:]:
+        fetch.start()
     heard = count_y + 2 + jnp.where(below, 6, 0) + jnp.where(above, 6, 0)
     fetches[0].wait()
     pl.semaphore_wait(barrier, heard)
@@ -386,8 +389,6 @@
             )
     for target in targets:
         guarded(target[4], lambda target=target: unit_send(*target[:4]))
-    phys_copy = pltpu.make_async_copy(phys, phys_far, near_sem.at[7])
-    phys_copy.start()
 
     lane = lax.broadcasted_iota(jnp.int32, (8, 128), 1)
     row = lax.broadcasted_iota(jnp.int32, (8, 128), 0)
@@ -609,7 +610,7 @@
     final = jnp.where(own, final, 0.0)
     last[...] = final
     whole[at_y] = final
-    for step in range(1, count_y):
+    for step in far_first:
         remote(last, whole.at[at_y], whole_sem.at[0], whole_sem.at[1], at_x, beside_y(step)).start()
 
     wait(halo.at[pl.ds(1, 4), pl.ds(0, 16)], halo_out.at[1])
@@ -622,7 +623,6 @@
         guarded(there, lambda: wait(units.at[2, some], unit_out.at[out_index]))
     for turn_index in range(2):
         node_wait(turn_index, node_out, True)
-    phys_copy.wait()
 
     wait(whole.at[pl.ds(0, count_y - 1)], whole_sem.at[1])
     columns = []
@@ -635,10 +635,7 @@
     across = jnp.concatenate(columns, axis=0).T
     for comp in range(3):
         sol[comp, :, 0, :] = across[GAP * comp : GAP * comp + 33, 0 : 4 * count_y + 1]
-    sol_copy = pltpu.make_async_copy(sol, sol_far, near_sem.at[8])
-    sol_copy.start()
     wait(whole.at[pl.ds(0, count_y - 1)], whole_sem.at[0])
-    sol_copy.wait()
 
 
 def solution(mesh):
@@ -647,6 +644,7 @@
 
     def body(density, passive, element_load):
         far = pl.BlockSpec(memory_space=pl.ANY)
+        near = pl.BlockSpec(memory_space=pltpu.VMEM)
         dma = pltpu.SemaphoreType.DMA
         across_shape = (3, 33, 1, 4 * count_y + 1)
 
@@ -663,10 +661,8 @@
                 jax.ShapeDtypeStruct(across_shape, jnp.float32),
             ),
             in_specs=[far] * 7,
-            out_specs=(far, far),
+            out_specs=(near, near),
             scratch_shapes=[
-                pltpu.VMEM(density.shape, jnp.float32),
-                pltpu.VMEM(across_shape, jnp.float32),
                 pltpu.VMEM((6, 32, 128), jnp.float32),
                 pltpu.VMEM(passive.shape, jnp.int32),
                 pltpu.VMEM(element_load.shape, jnp.float32),
@@ -681,7 +677,7 @@
                 pltpu.VMEM((128, 128), jnp.bfloat16),
                 pltpu.VMEM((256, 1024), jnp.bfloat16),
                 pltpu.VMEM((24, 8, 128), jnp.float32),
-                dma((9,)),
+                dma((7,)),
                 dma((3,)),
                 dma((3,)),
                 dma((6,)),
@@ -694,6 +690,27 @@
             ],
             compiler_params=pltpu.CompilerParams(collective_id=0, has_side_effects=True, vmem_limit_bytes=16 * 2**20),
         )(*[pltpu.with_memory_space_constraint(operand, pltpu.HBM) for operand in operands])
+        def settle(physical_from, across_from, physical_to, across_to, sems):
+            copies = [
+                pltpu.make_async_copy(physical_from, physical_to, sems.at[0]),
+                pltpu.make_async_copy(across_from, across_to, sems.at[1]),
+            ]
+            for copy in copies:
+                copy.start()
+            for copy in copies:
+                copy.wait()
+
+        physical, across = pl.pallas_call(
+            settle,
+            out_shape=(
+                jax.ShapeDtypeStruct(density.shape, jnp.float32),
+                jax.ShapeDtypeStruct(across_shape, jnp.float32),
+            ),
+            in_specs=[far, far],
+            out_specs=(far, far),
+            scratch_shapes=[dma((2,))],
+            compiler_params=pltpu.CompilerParams(vmem_limit_bytes=2**20),
+        )(physical, across)
         return physical, across.transpose(0, 2, 3, 1)
 
     return jax.shard_map(

time: 37.6 us -> 36.8 us (0.979)
  local copies, waits for them, and re-layouts: 1.24 us -> 0 us
  Pallas kernels: 35.6 us -> 36.1 us
    unnamed x2 -> x0, local copies, waits for them, and re-layouts: 1.24 us -> none
    pallas_call x0 -> x1, Pallas kernels: none -> 0.65 us  [body(): pl.pallas_call(settle, out_shape=(jax.ShapeDtypeStruct(density.shape, jnp...]
where the time goes in v3:
time: 36.8 us; the launch traced here: 36.7 us
  Pallas kernels  36.1 us (98%)
  between operations  0.64 us (2%)
    pallas_call x1, Pallas kernels, body(): pl.pallas_call(run, out_shape=(jax.ShapeDtypeStruct(density.shape, jnp.fl...  35.4 us

profile of v3, /device:TPU:65, one launch (start us, length us, event | category | flops | bytes accessed | tf_op | source)
XLA Modules:
  0.0 36.7 jit_solution(7126389311309666574)
XLA Ops:
  0.6 35.4 %shard_map.104 = (f32[4,16,128]{2,1,0:T(8,128)S(1)}, f32[3,33,1,65]{3,2,1,0:T(1,128)S(1)}) custom-call(f32[4,16,128]{2,1,0:T(8,128)} %refs_0_.1, s32[4,16,128]{2,1,0:T(8,128)} %refs_1_.1, f32[24,1,4,32]{3,2,1,0:T(4,128)} %refs_2_.1, bf16[544,512]{1,0:T(8,128)(2,1)} %constant.19.refs_3_, bf16[64,512]{1,0:T(8,128)(2,1)} %constant.24.refs_4_, ...), custom_call_target="tpu_custom_call" | custom-call | tf_op jit(solution)/shard_map/pallas_call | solution.py:657
  36.1 0.7 %shard_map.105 = (f32[4,16,128]{2,1,0:T(8,128)}, f32[3,33,1,65]{3,2,1,0:T(1,128)}) custom-call(f32[4,16,128]{2,1,0:T(8,128)S(1)} %get-tuple-element.6.physical_from, f32[3,33,1,65]{3,2,1,0:T(1,128)S(1)} %get-tuple-element.7.across_from), custom_call_target="tpu_custom_call" | custom-call | tf_op jit(solution)/shard_map/pallas_call | solution.py:703

commit v4 on v3

--- a/solution.py
+++ b/solution.py
@@ -514,15 +514,13 @@
     build(3, terms(full, 0, parts[3]) + terms(full, 1, parts[2]))
     scale[3] = scale_of(3)
     guarded(below, lambda: wait(units.at[1], unit_in.at[3]))
-    parts[1] = around(1)
+    guarded(below, lambda: wait(units.at[0], unit_in.at[2]))
+    guarded(above, lambda: wait(units.at[4], unit_in.at[4]))
+    for layer in (1, 0, 4):
+        parts[layer] = around(layer)
+    for layer in (1, 4, 2):
+        scale[layer] = scale_of(layer)
     build(2, terms(full, 0, parts[2]) + terms(full, 1, parts[1]))
-    scale[2] = scale_of(2)
-    guarded(below, lambda: wait(units.at[0], unit_in.at[2]))
-    parts[0] = around(0)
-    scale[1] = scale_of(1)
-    guarded(above, lambda: wait(units.at[4], unit_in.at[4]))
-    parts[4] = around(4)
-    scale[4] = scale_of(4)
 
     def entry(layer, index):
         return stencil[layer - 1, 8 * index : 8 * index + 8, :]

time: 36.8 us -> 36.2 us (0.984)
  Pallas kernels: 36.1 us -> 35.4 us
    pallas_call x1, Pallas kernels: 35.4 us -> 34.8 us  [body(): pl.pallas_call(run, out_shape=(jax.ShapeDtypeStruct(density.shape, jnp.fl...]
where the time goes in v4:
time: 36.2 us; the launch traced here: 36.1 us
  Pallas kernels  35.4 us (98%)
  between operations  0.64 us (2%)
    pallas_call x1, Pallas kernels, body(): pl.pallas_call(run, out_shape=(jax.ShapeDtypeStruct(density.shape, jnp.fl...  34.8 us

profile of v4, /device:TPU:65, one launch (start us, length us, event | category | flops | bytes accessed | tf_op | source)
XLA Modules:
  0.0 36.1 jit_solution(17274493399945475034)
XLA Ops:
  0.6 34.8 %shard_map.104 = (f32[4,16,128]{2,1,0:T(8,128)S(1)}, f32[3,33,1,65]{3,2,1,0:T(1,128)S(1)}) custom-call(f32[4,16,128]{2,1,0:T(8,128)} %refs_0_.1, s32[4,16,128]{2,1,0:T(8,128)} %refs_1_.1, f32[24,1,4,32]{3,2,1,0:T(4,128)} %refs_2_.1, bf16[544,512]{1,0:T(8,128)(2,1)} %constant.19.refs_3_, bf16[64,512]{1,0:T(8,128)(2,1)} %constant.24.refs_4_, ...), custom_call_target="tpu_custom_call" | custom-call | tf_op jit(solution)/shard_map/pallas_call | solution.py:655
  35.4 0.7 %shard_map.105 = (f32[4,16,128]{2,1,0:T(8,128)}, f32[3,33,1,65]{3,2,1,0:T(1,128)}) custom-call(f32[4,16,128]{2,1,0:T(8,128)S(1)} %get-tuple-element.6.physical_from, f32[3,33,1,65]{3,2,1,0:T(1,128)S(1)} %get-tuple-element.7.across_from), custom_call_target="tpu_custom_call" | custom-call | tf_op jit(solution)/shard_map/pallas_call | solution.py:701

commit v5 on v4

--- a/solution.py
+++ b/solution.py
@@ -513,19 +513,25 @@
     parts[3] = around(3)
     build(3, terms(full, 0, parts[3]) + terms(full, 1, parts[2]))
     scale[3] = scale_of(3)
+    half_2 = terms(full, 0, parts[2])
     guarded(below, lambda: wait(units.at[1], unit_in.at[3]))
     guarded(below, lambda: wait(units.at[0], unit_in.at[2]))
     guarded(above, lambda: wait(units.at[4], unit_in.at[4]))
     for layer in (1, 0, 4):
         parts[layer] = around(layer)
+    own_2 = half_2 + terms(full, 1, parts[1])
     for layer in (1, 4, 2):
         scale[layer] = scale_of(layer)
-    build(2, terms(full, 0, parts[2]) + terms(full, 1, parts[1]))
+    build(2, own_2)
 
     def entry(layer, index):
         return stencil[layer - 1, 8 * index : 8 * index + 8, :]
 
-    def sweep(tiles, layer):
+    def chosen(values, layer):
+        return jnp.where(half_x == 0, values[layer], values[layer + 1])
+
+    def sweep(tiles, layer, single=False):
+        spot = layer + half_x if single else layer
         sums = [None, None, None]
         for step_x in range(3):
             for step_z in range(3):
@@ -534,7 +540,7 @@
                     moved = turn(moved_z, 1 - step_y, 0)
                     for comp in range(3):
                         index = 27 * comp + 9 * step_x + 3 * step_y + step_z
-                        term = entry(layer, index) * moved
+                        term = entry(spot, index) * moved
                         sums[comp] = term if sums[comp] is None else sums[comp] + term
         product = jnp.where(
             groups[0],
@@ -545,8 +551,9 @@
                 sums[2] + turn(sums[2], GAP, 1) + turn(sums[2], 2 * GAP, 1),
             ),
         )
-        factor = scale[layer]
-        updated = tiles[layer] + factor * (right_side[layer - 1] - product)
+        factor = chosen(scale, layer) if single else scale[layer]
+        given = chosen(right_side, layer - 1) if single else right_side[layer - 1]
+        updated = tiles[layer] + factor * (given - product)
         return jnp.where(factor > 0.0, updated, 0.0)
 
     def first(layer):
@@ -600,12 +607,14 @@
                 ),
                 layer,
             )
-        later = {layer: sweep(tiles, layer) for layer in range(1, 5)}
-        if turn_index == 0:
+        if turn_index == 1:
+            tiles = {layer: chosen(tiles, layer) for layer in range(5)}
+            later = {layer: sweep(tiles, layer, True) for layer in range(1, 4)}
+        else:
+            later = {layer: sweep(tiles, layer) for layer in range(1, 5)}
             pair_now = [jnp.where(own, sweep(later, layer), 0.0) for layer in (2, 3)]
 
-    final = jnp.where(half_x == 0, sweep(later, 2), sweep(later, 3))
-    final = jnp.where(own, final, 0.0)
+    final = jnp.where(own, sweep(later, 2, True), 0.0)
     last[...] = final
     whole[at_y] = final
     for step in far_first:

time: 36.2 us -> 36 us (level)
  no operation moved by 1% of the time
where the time goes in v5:
time: 36 us; the launch traced here: 35.9 us
  Pallas kernels  35.2 us (98%)
  between operations  0.64 us (2%)
    pallas_call x1, Pallas kernels, body(): pl.pallas_call(run, out_shape=(jax.ShapeDtypeStruct(density.shape, jnp.fl...  34.6 us

profile of v5, /device:TPU:65, one launch (start us, length us, event | category | flops | bytes accessed | tf_op | source)
XLA Modules:
  0.0 35.9 jit_solution(1560660312739565799)
XLA Ops:
  0.6 34.6 %shard_map.104 = (f32[4,16,128]{2,1,0:T(8,128)S(1)}, f32[3,33,1,65]{3,2,1,0:T(1,128)S(1)}) custom-call(f32[4,16,128]{2,1,0:T(8,128)} %refs_0_.1, s32[4,16,128]{2,1,0:T(8,128)} %refs_1_.1, f32[24,1,4,32]{3,2,1,0:T(4,128)} %refs_2_.1, bf16[544,512]{1,0:T(8,128)(2,1)} %constant.19.refs_3_, bf16[64,512]{1,0:T(8,128)(2,1)} %constant.24.refs_4_, ...), custom_call_target="tpu_custom_call" | custom-call | tf_op jit(solution)/shard_map/pallas_call | solution.py:664
  35.2 0.7 %shard_map.105 = (f32[4,16,128]{2,1,0:T(8,128)}, f32[3,33,1,65]{3,2,1,0:T(1,128)}) custom-call(f32[4,16,128]{2,1,0:T(8,128)S(1)} %get-tuple-element.6.physical_from, f32[3,33,1,65]{3,2,1,0:T(1,128)S(1)} %get-tuple-element.7.across_from), custom_call_target="tpu_custom_call" | custom-call | tf_op jit(solution)/shard_map/pallas_call | solution.py:710
